TPU v7x, 512 devices: a whole 4x4x16 slice. The times are simulated.
512 devices in a mesh: grp: 16 (over y, z_hi, core), dev: 32 (over x, z_lo).
Axes of the slice: x: 4, y: 4, z: 16 (z_hi: 2, z_lo: 8; z = z_hi * 8 + z_lo), core: 2. Of those that a mesh axis runs over, the one named last changes fastest.
Arguments:
- colloc: bfloat16 [12288, 8000], P('dev', 'grp'), may hold values from -3 to 3
- block_colloc: bfloat16 [1024, 8000], P('dev', 'grp'), may hold values from -3 to 3
- factor: float32 [12288, 8192], P('dev', 'grp'), may hold values from -4.8 to 4.8
- block_factor: float32 [1024, 8192], P('dev', 'grp'), may hold values from -0.25 to 0.25
Outputs:
- block_lower: float32 [1024, 1024], P('dev')
- panel_lower: float32 [32, 384, 1024], P('dev', 'grp')
All inputs are finite; a program needn't handle non-finite values.
Results may differ from a plain program's by a relative error of at most 0.0003.
Values may be sent and summed in bfloat16 or wider, within the bound.
A program may use at most 64 MiB of HBM per device.

v0:
```python
import jax
import jax.numpy as jnp
from jax import lax
from jax.sharding import PartitionSpec as P

DAMPING = 0.0625


def copy_for_each(x, axis):
    copies = jnp.broadcast_to(x, (lax.axis_size(axis), *x.shape))
    return lax.all_to_all(copies, axis, split_axis=0, concat_axis=0, tiled=True)


def joined_along(tiles, dim):
    dims = list(tiles.shape[1:])
    dims[dim] *= tiles.shape[0]
    return jnp.moveaxis(tiles, 0, dim).reshape(dims)


def gathered_copies(x, axis, dim):
    tiles = copy_for_each(x, axis)
    return joined_along(tiles, dim)


def in_one_piece(arrays, axis, dim, along):
    widths = [a.shape[along] for a in arrays]
    both = jnp.concatenate(arrays, axis=along)
    out = lax.psum_scatter(both, axis, scatter_dimension=dim, tiled=True)
    return tuple(jnp.split(out, [sum(widths[:k]) for k in range(1, len(widths))], axis=along))


def with_damping(gram_part, update_part, row_index, col_index):
    return (
        gram_part * gram_part
        + jnp.where(row_index == col_index, jnp.float32(DAMPING), jnp.float32(0.0))
        - update_part
    )


def on_device(colloc, block_colloc, factor, block_factor):
    grp_count = lax.axis_size("grp")
    grp_index = lax.axis_index("grp")
    dev_index = lax.axis_index("dev")
    band_rows = block_colloc.shape[0]
    panel_width = band_rows * lax.axis_size("dev")
    points = jnp.concatenate([block_colloc, colloc], axis=0)
    earlier = jnp.concatenate([block_factor, factor], axis=0)
    metric_terms = lax.dot_general(
        points,
        gathered_copies(block_colloc, "dev", 0),
        (((1,), (1,)), ((), ())),
        preferred_element_type=jnp.float32,
    )
    update_terms = lax.dot_general(
        earlier,
        gathered_copies(block_factor, "dev", 0),
        (((1,), (1,)), ((), ())),
        precision=lax.Precision.HIGHEST,
        preferred_element_type=jnp.float32,
    )
    gram_low, update_low = in_one_piece(
        (metric_terms[band_rows:], update_terms[band_rows:]), "grp", 0, 1
    )
    below_rows = gram_low * gram_low - update_low
    gram_head = metric_terms[:band_rows]
    update_head = update_terms[:band_rows]
    row_index = dev_index * band_rows + lax.broadcasted_iota(jnp.int32, (band_rows, 1), 0)
    slice_width = panel_width // grp_count
    slice_index = grp_index * slice_width + lax.broadcasted_iota(jnp.int32, (1, slice_width), 1)
    gram_slice, update_slice = in_one_piece((gram_head, update_head), "grp", 1, 0)
    own_slice = with_damping(gram_slice, update_slice, row_index, slice_index)
    column_slab = gathered_copies(own_slice, "dev", 0)
    schur = lax.all_gather(column_slab, "grp", axis=1, tiled=True)
    cholesky_factor = jnp.linalg.cholesky(schur)
    panel_rows = lax.linalg.triangular_solve(
        cholesky_factor, below_rows, left_side=False, lower=True, transpose_a=True
    )
    factor_rows = lax.dynamic_slice_in_dim(cholesky_factor, dev_index * band_rows, band_rows, 0)
    return (factor_rows, panel_rows[None])


def solution(mesh):
    placed = (P("dev", "grp"), P("dev", "grp"), P("dev", "grp"), P("dev", "grp"))
    return jax.shard_map(
        on_device,
        mesh=mesh,
        in_specs=placed,
        out_specs=(P("dev", None), P("dev", "grp", None)),
        check_vma=False,
    )
```

profile of v0, /device:TPU:25, one launch (start us, length us, event | category | flops | bytes accessed | tf_op | source)
XLA Modules:
  0.0 870.8 jit_solution(12933287976333306177)
XLA Ops:
  8.1 65.3 %all_to_all.15 = bf16[32,32,500]{2,1,0:T(8,128)(2,1)S(1)} all-to-all(bf16[32,32,500]{2,1,0:T(8,128)(2,1)S(1)} %broadcast_in_dim.22), channel_id=1, replica_groups=mesh['grp'=16,'dev'=32] {'dev'}, dimensions={0} | all-to-all | bytes 2048000 | tf_op jit(solution)/shard_map/all_to_all | solution.py:11
  73.4 2.5 broadcast_in_dim.23
  75.8 6.4 all-to-all-start.1
  82.5 2.1 fusion.11
  84.6 1.2 copy-done.1
  85.8 89.0 %all-to-all-done.1 = f32[32,32,512]{2,1,0:T(8,128)S(1)} async-done(((f32[32,32,512]{2,1,0:T(8,128)}), f32[32,32,512]{2,1,0:T(8,128)S(1)}, u32[]{:S(2)}, u32[]{:S(2)}) %all-to-all-start.1) | async-done | bytes 2097184 | tf_op jit(solution)/shard_map/all_to_all | solution.py:11
  174.9 4.1 fusion.5
  179.0 1.2 copy-done.2
  182.3 1.9 pad_maximum_fusion
  184.3 96.0 %reduce-scatter.7.cloned.1.call-done = f32[64,64]{1,0:T(8,128)} async-done(((f32[1024,64]{1,0:T(8,128)}), f32[64,64]{1,0:T(8,128)}) %reduce-scatter.7.cloned.1.call-update) | async-done | bytes 16400
  281.8 22.6 %all_to_all.16 = f32[32,1,2048]{2,1,0:T(1,128)S(1)} all-to-all(f32[32,1,2048]{2,1,0:T(1,128)S(1)} %reshape.118), channel_id=1, replica_groups=mesh['grp'=16,'dev'=32] {'dev'}, dimensions={0} | all-to-all | bytes 524288 | tf_op jit(solution)/shard_map/all_to_all | solution.py:11
  304.8 1.3 reduce.48
  307.2 106.5 %reduce-scatter.5.cloned.1.call-done = f32[24,2048]{1,0:T(8,128)} async-done(((f32[384,2048]{1,0:T(8,128)}), f32[24,2048]{1,0:T(8,128)}) %reduce-scatter.5.cloned.1.call-update) | async-done | bytes 196624 | tf_op jit(solution)/shard_map/reduce_scatter | solution.py:28
  414.7 112.9 %all-gather.2.cloned.1.call-done = f32[1024,1024]{0,1:T(8,128)} async-done(((f32[1024,64]{0,1:T(8,128)}), f32[1024,1024]{0,1:T(8,128)}) %all-gather.2.cloned.1.call-update) | async-done | bytes 4194320 | tf_op jit(solution)/shard_map/all_gather | solution.py:73
  527.6 5.8 copy.14
  533.4 4.4 fusion
  537.9 1.9 copy-done
  539.8 11.7 %cholesky.223 = f32[128,128]{1,0:T(8,128)S(1)} custom-call(f32[128,128]{1,0:T(8,128)S(1)} %cholesky.580), custom_call_target="Cholesky" | custom-call | tf_op jit(solution)/shard_map/jit(cholesky)/cholesky | solution.py:74
  551.6 9.8 %custom-call.62 = f32[1,128,128]{1,2,0:T(8,128)S(1)} custom-call(f32[1,128,128]{2,1,0:T(8,128)S(1)} %get-tuple-element.43), custom_call_target="InvertDiagBlocksLowerTriangular" | custom-call | tf_op jit(solution)/shard_map/jit(cholesky)/cholesky | solution.py:74
  561.4 2.5 cholesky.255
  563.9 2.3 constant_dynamic-update-slice_fusion.32
  566.2 1.5 convolution_subtract_fusion
  567.8 11.9 %cholesky.244 = f32[128,128]{1,0:T(8,128)S(1)} custom-call(f32[128,128]{1,0:T(8,128)S(1)} %cholesky.584), custom_call_target="Cholesky" | custom-call | tf_op jit(solution)/shard_map/jit(cholesky)/cholesky | solution.py:74
  580.3 9.8 %custom-call.63 = f32[1,128,128]{1,2,0:T(8,128)S(1)} custom-call(f32[1,128,128]{2,1,0:T(8,128)S(1)} %get-tuple-element.40), custom_call_target="InvertDiagBlocksLowerTriangular" | custom-call | tf_op jit(solution)/shard_map/jit(cholesky)/cholesky | solution.py:74
  590.1 1.2 convolution_dynamic-update-slice_fusion
  591.4 2.1 convolution_subtract_fusion.1
  593.5 11.7 %cholesky.468 = f32[128,128]{1,0:T(8,128)S(1)} custom-call(f32[128,128]{1,0:T(8,128)S(1)} %cholesky.589), custom_call_target="Cholesky" | custom-call | tf_op jit(solution)/shard_map/jit(cholesky)/cholesky | solution.py:74
  606.5 9.8 %custom-call.64 = f32[1,128,128]{1,2,0:T(8,128)S(1)} custom-call(f32[1,128,128]{2,1,0:T(8,128)S(1)} %get-tuple-element.37), custom_call_target="InvertDiagBlocksLowerTriangular" | custom-call | tf_op jit(solution)/shard_map/jit(cholesky)/cholesky | solution.py:74
  616.3 1.2 convolution_dynamic-update-slice_fusion.1
  617.5 2.3 convolution_subtract_fusion.2
  619.8 11.9 %cholesky.487 = f32[128,128]{1,0:T(8,128)S(1)} custom-call(f32[128,128]{1,0:T(8,128)S(1)} %cholesky.594), custom_call_target="Cholesky" | custom-call | tf_op jit(solution)/shard_map/jit(cholesky)/cholesky | solution.py:74
  633.0 9.8 %custom-call.65 = f32[1,128,128]{1,2,0:T(8,128)S(1)} custom-call(f32[1,128,128]{2,1,0:T(8,128)S(1)} %get-tuple-element.34), custom_call_target="InvertDiagBlocksLowerTriangular" | custom-call | tf_op jit(solution)/shard_map/jit(cholesky)/cholesky | solution.py:74
  642.8 1.1 convolution_dynamic-update-slice_fusion.2
  643.9 2.3 convolution_subtract_fusion.3
  646.3 11.7 %cholesky.506 = f32[128,128]{1,0:T(8,128)S(1)} custom-call(f32[128,128]{1,0:T(8,128)S(1)} %cholesky.599), custom_call_target="Cholesky" | custom-call | tf_op jit(solution)/shard_map/jit(cholesky)/cholesky | solution.py:74
  659.4 10.2 %custom-call.66 = f32[1,128,128]{1,2,0:T(8,128)S(1)} custom-call(f32[1,128,128]{2,1,0:T(8,128)S(1)} %get-tuple-element.31), custom_call_target="InvertDiagBlocksLowerTriangular" | custom-call | tf_op jit(solution)/shard_map/jit(cholesky)/cholesky | solution.py:74
  669.6 1.0 convolution_dynamic-update-slice_fusion.3
  670.6 2.3 convolution_subtract_fusion.4
  672.9 11.7 %cholesky.526 = f32[128,128]{1,0:T(8,128)S(1)} custom-call(f32[128,128]{1,0:T(8,128)S(1)} %cholesky.604), custom_call_target="Cholesky" | custom-call | tf_op jit(solution)/shard_map/jit(cholesky)/cholesky | solution.py:74
  685.9 9.8 %custom-call.67 = f32[1,128,128]{1,2,0:T(8,128)S(1)} custom-call(f32[1,128,128]{2,1,0:T(8,128)S(1)} %get-tuple-element.28), custom_call_target="InvertDiagBlocksLowerTriangular" | custom-call | tf_op jit(solution)/shard_map/jit(cholesky)/cholesky | solution.py:74
  696.7 2.0 convolution_subtract_fusion.5
  698.7 11.9 %cholesky.546 = f32[128,128]{1,0:T(8,128)S(1)} custom-call(f32[128,128]{1,0:T(8,128)S(1)} %cholesky.609), custom_call_target="Cholesky" | custom-call | tf_op jit(solution)/shard_map/jit(cholesky)/cholesky | solution.py:74
  711.9 9.8 %custom-call.68 = f32[1,128,128]{1,2,0:T(8,128)S(1)} custom-call(f32[1,128,128]{2,1,0:T(8,128)S(1)} %get-tuple-element.25), custom_call_target="InvertDiagBlocksLowerTriangular" | custom-call | tf_op jit(solution)/shard_map/jit(cholesky)/cholesky | solution.py:74
  722.5 1.8 convolution_subtract_fusion.6
  724.3 11.7 %cholesky.564 = f32[128,128]{1,0:T(8,128)S(1)} custom-call(f32[128,128]{1,0:T(8,128)S(1)} %convolution_subtract_fusion.6), custom_call_target="Cholesky" | custom-call | tf_op jit(solution)/shard_map/jit(cholesky)/cholesky | solution.py:74
  743.0 6.6 fusion.1
  749.6 23.2 %while.1 = (s32[]{:T(128)}, f32[1024,1024]{1,0:T(8,128)}, s32[8,2]{0,1:T(2,128)S(1)}, f32[8,128,128]{2,1,0:T(8,128)S(1)}, s32[]{:T(128)}) while((s32[]{:T(128)}, f32[1024,1024]{1,0:T(8,128)}, s32[8,2]{0,1:T(2,128)S(1)}, f32[8,128,128]{2,1,0:T(8,128)S(1)}, s32[]{:T(128)}) %tuple.63), condition=%wide.while_cond, body=%wide.while_body.sunk | while | flops 2 | bytes 131189 | solution.py:75
  750.2 2.3 bitcast_dynamic-update-slice_fusion.2
  753.1 2.3 bitcast_dynamic-update-slice_fusion.2
  756.0 2.3 bitcast_dynamic-update-slice_fusion.2
  758.9 2.3 bitcast_dynamic-update-slice_fusion.2
  761.8 2.3 bitcast_dynamic-update-slice_fusion.2
  764.7 2.3 bitcast_dynamic-update-slice_fusion.2
  767.6 2.3 bitcast_dynamic-update-slice_fusion.2
  770.5 2.2 bitcast_dynamic-update-slice_fusion.2
  772.8 78.6 %custom-call.69 = f32[8,128,128]{1,2,0:T(8,128)S(1)} custom-call(f32[8,128,128]{2,1,0:T(8,128)S(1)} %get-tuple-element.9), custom_call_target="InvertDiagBlocksLowerTriangular" | custom-call | tf_op jit(solution)/shard_map/triangular_solve | solution.py:75
  851.6 1.0 convolution_subtract_fusion.10
  852.8 1.1 convolution_subtract_fusion.9
  854.1 1.2 convolution_subtract_fusion.8
  855.5 1.2 convolution_subtract_fusion.7
  857.0 1.4 convolution_subtract_fusion.13
  858.6 1.4 convolution_subtract_fusion.12
  860.2 1.5 convolution_subtract_fusion.11
  861.7 1.6 constant_dynamic-slice_fusion.1
  (88 shorter events, 25.0 us)
Async XLA Ops:
  8.0 74.3 %copy-start.4 = (bf16[32,500]{1,0:T(8,128)(2,1)S(1)}, bf16[32,500]{1,0:T(8,128)(2,1)}, u32[]{:S(2)}) copy-start(bf16[32,500]{1,0:T(8,128)(2,1)} %param.5) | copy-start | bytes 96004
  75.8 99.0 %copy-start.3 = (f32[32,512]{1,0:T(8,128)S(1)}, f32[32,512]{1,0:T(8,128)}, u32[]{:S(2)}) copy-start(f32[32,512]{1,0:T(8,128)} %param.7) | copy-start | bytes 196612
  75.8 99.0 %all-to-all-start.1 = ((f32[32,32,512]{2,1,0:T(8,128)}), f32[32,32,512]{2,1,0:T(8,128)S(1)}, u32[]{:S(2)}, u32[]{:S(2)}) async-start(f32[32,32,512]{2,1,0:T(8,128)} %broadcast_in_dim.23), calls=%async_computation.1 | async-start | bytes 4194304 | tf_op jit(solution)/shard_map/all_to_all | solution.py:11
  82.3 197.9 %reduce-scatter.7.cloned.1.call-start = ((), (), s32[]{:S(2)}) async-start(), calls=%async_computation.7 | async-start | bytes 557056
  84.6 1.2 copy-start.1
  179.0 1.2 copy-start.2
  180.2 1.6 slice-start
  180.2 2.1 slice-start.1
  181.3 232.5 %reduce-scatter.5.cloned.1.call-start = ((), (), s32[]{:S(2)}) async-start(), calls=%async_computation.6 | async-start | bytes 3342336 | tf_op jit(solution)/shard_map/reduce_scatter | solution.py:28
  184.2 343.5 %all-gather.2.cloned.1.call-start = ((), (), s32[]{:S(2)}) async-start(), calls=%async_computation.5 | async-start | bytes 4456448 | tf_op jit(solution)/shard_map/all_gather | solution.py:73
  537.9 1.9 copy-start
  863.5 0.7 copy-start.5
Sparse Core Ops, SparseCore 0:
  181.4 98.7 reduce-scatter.6
  285.1 128.6 reduce-scatter.4
  417.1 110.5 all-gather.1
where the time goes:
time: 881 us; the launch traced here: 871 us
  waiting for transfers between devices  405 us (46%)
  other arithmetic  266 us (30%)
  blocking collectives  87.9 us (10%)
  local copies, waits for them, and re-layouts  46.4 us (5%)
  matrix products  39.5 us (4%)
  between operations  19.6 us (2%)
    another operation x30, other arithmetic, on_device(): cholesky_factor = jnp.linalg.cholesky(schur)  172 us
    all_gather x1, waiting for transfers between devices, on_device(): schur = lax.all_gather(column_slab, 'grp', axis=1, tiled=True)  113 us
    reduce_scatter x1, waiting for transfers between devices, in_one_piece(): out = lax.psum_scatter(both, axis, scatter_dimension=dim, tiled=True)  107 us
    unnamed x4, waiting for transfers between devices  96 us
    all_to_all x1, waiting for transfers between devices, copy_for_each(): return lax.all_to_all(copies, axis, split_axis=0, concat_axis=0, tiled=True)  89 us
    all_to_all x2, blocking collectives, copy_for_each(): return lax.all_to_all(copies, axis, split_axis=0, concat_axis=0, tiled=True)  87.9 us
    another operation x3, other arithmetic, on_device(): lax.linalg.triangular_solve(cholesky_factor, below_rows, left_side=False,...  85.2 us
    another operation x14, matrix products, on_device(): cholesky_factor = jnp.linalg.cholesky(schur)  23 us
  transfers between devices with their start and end apart: 4, of which 4 were waited for; matrix products, arithmetic and copies ran while one was open for 1% of the time, Pallas kernels for 0%

commit v1 on v0

v1 whole, which is shorter than its diff:
```python
import functools

import jax
import jax.numpy as jnp
from jax import lax
from jax.experimental import pallas as pl
from jax.experimental.pallas import tpu as pltpu
from jax.sharding import PartitionSpec as P

DAMPING = 0.0625
HI = lax.Precision.HIGHEST
MESH = pl.DeviceIdType.MESH
F32 = jnp.float32
VMEM = pl.BlockSpec(memory_space=pltpu.VMEM)


def dot(a, b, ca, cb, precision=None):
    return lax.dot_general(a, b, (((ca,), (cb,)), ((), ())), precision=precision, preferred_element_type=F32)


def place(x, y, zl, zh, c):
    return {"grp": y * 4 + zh * 2 + c, "dev": x * 8 + zl}


def exchange(bc, bf, bca, bfa, sb, xbc, xbf, part, rcore, acc, ry, s2, rz,
             zr, zs, xr, xs, br, bs, cr, cs, yr, ys, hr, hs, pr, ps, ar, as_, dr, ds, er, es):
    g = lax.axis_index("grp")
    d = lax.axis_index("dev")
    y, zh, c = g // 4, (g // 2) % 2, g % 2
    x, zl = d // 8, d % 8
    sent = []

    def push(src, dst, ssem, rsem, to, when=None):
        def make():
            return pltpu.make_async_remote_copy(
                src_ref=src(), dst_ref=dst(), send_sem=ssem, recv_sem=rsem, device_id=to(), device_id_type=MESH
            )

        if when is None:
            make().start()
        else:
            pl.when(when)(lambda: make().start())
        sent.append((when, make))

    def arrived(ref, ssem, rsem):
        pltpu.make_async_remote_copy(
            src_ref=ref, dst_ref=ref, send_sem=ssem, recv_sem=rsem,
            device_id=place(x, y, zl, zh, 1 - c), device_id_type=MESH,
        ).wait_recv()

    barrier = pltpu.get_barrier_semaphore()
    ring = [(zl + k % 8) % 8 for k in range(16)]
    half = [(zh + k // 8) % 2 for k in range(16)]
    peers = [place(x, y, zl, zh, 1 - c)]
    peers += [place(x, y, ring[k], half[k], c) for k in range(1, 16)]
    peers += [place((x + k) % 4, y, zl, zh, c) for k in range(1, 4)]
    peers += [place(x, (y + k) % 4, zl, zh, c) for k in range(1, 4)]
    for peer in peers:
        pl.semaphore_signal(barrier, inc=1, device_id=peer, device_id_type=MESH)
    pl.semaphore_wait(barrier, len(peers))

    chunks = [
        (bc, lambda slot: bca.at[slot]),
        (bf.at[0:16], lambda slot: bfa.at[slot, 0:16]),
        (bf.at[16:32], lambda slot: bfa.at[slot, 16:32]),
    ]
    for q, (own, at) in enumerate(chunks):
        for way, step in ((0, 1), (1, -1)):
            ok = (zl < 7) if step == 1 else (zl > 0)
            push(lambda own=own: own, lambda at=at: at(d), zs.at[q, 0, way], zr.at[q, zl],
                 lambda step=step: place(x, y, zl + step, zh, c), ok)
    for k in range(1, 4):
        to = lambda k=k: place((x + k) % 4, y, zl, zh, c)
        push(lambda: bc, lambda: xbc.at[x], xs.at[0, k - 1], xr.at[0, k - 1], to)
        push(lambda: bf, lambda: xbf.at[x], xs.at[1, k - 1], xr.at[1, k - 1], to)
    bca[d] = bc[...]
    bfa[d] = bf[...]
    xbc[x] = bc[...]
    xbf[x] = bf[...]
    for s in range(1, 8):
        for q, (own, at) in enumerate(chunks):
            for way, step in ((0, 1), (1, -1)):
                src = zl - step * s
                inside = (src >= 0) if step == 1 else (src <= 7)
                more = (zl < 7) if step == 1 else (zl > 0)

                @pl.when(inside)
                def _(at=at, src=src, q=q):
                    arrived(at(x * 8 + src), zs.at[q, 0, 0], zr.at[q, src])

                if s < 7:
                    push(lambda at=at, src=src: at(x * 8 + src), lambda at=at, src=src: at(x * 8 + src),
                         zs.at[q, s, way], zr.at[q, src],
                         lambda step=step: place(x, y, zl + step, zh, c), jnp.logical_and(inside, more))
    mine = pl.ds(x * 8, 8)
    for k in range(1, 4):
        to = lambda k=k: place((x + k) % 4, y, zl, zh, c)
        push(lambda: bca.at[mine], lambda: bca.at[mine], bs.at[0, k - 1], br.at[0, k - 1], to)
        push(lambda: bfa.at[mine], lambda: bfa.at[mine], bs.at[1, k - 1], br.at[1, k - 1], to)
    for k in range(1, 4):
        arrived(xbc.at[(x + 4 - k) % 4], xs.at[0, k - 1], xr.at[0, k - 1])
        arrived(xbf.at[(x + 4 - k) % 4], xs.at[1, k - 1], xr.at[1, k - 1])
    gram = dot(xbc[...].reshape(128, 500), bca[mine].reshape(256, 500), 1, 1)
    update = dot(xbf[...].reshape(128, 512), bfa[mine].reshape(256, 512), 1, 1, HI)
    for a in range(4):
        for b in range(2):
            for e in range(2):
                lo = a * 32 + b * 16 + e * 8
                part[b, a, e, 0] = gram[lo:lo + 8]
                part[b, a, e, 1] = update[lo:lo + 8]
    push(lambda: part.at[1 - c], lambda: rcore, cs, cr, lambda: place(x, y, zl, zh, 1 - c))
    arrived(rcore, cs, cr)
    acc[...] = part[c] + rcore[...]
    for k in range(1, 4):
        push(lambda k=k: acc.at[(y + k) % 4], lambda k=k: ry.at[k - 1], ys.at[k - 1], yr.at[k - 1],
             lambda k=k: place(x, (y + k) % 4, zl, zh, c))
    for k in range(1, 4):
        arrived(ry.at[k - 1], ys.at[k - 1], yr.at[k - 1])
    s2[...] = acc[y] + ry[0] + ry[1] + ry[2]
    push(lambda: s2.at[1 - zh], lambda: rz, hs, hr, lambda: place(x, y, zl, 1 - zh, c))
    arrived(rz, hs, hr)
    total = s2[zh] + rz[...]
    row = y * 256 + zl * 32 + c * 16 + zh * 8 + lax.broadcasted_iota(jnp.int32, (8, 256), 0)
    col = x * 256 + lax.broadcasted_iota(jnp.int32, (8, 256), 1)
    sb[x, y, c, zl, zh] = total[0] * total[0] + jnp.where(row == col, F32(DAMPING), F32(0.0)) - total[1]
    for k in range(1, 16):
        push(lambda: sb.at[x, y, c, zl, zh], lambda: sb.at[x, y, c, zl, zh], ps.at[k - 1], pr.at[k - 1],
             lambda k=k: place(x, y, ring[k], half[k], c))
    for k in range(1, 16):
        back_l, back_h = (zl + 8 - k % 8) % 8, (zh + k // 8) % 2
        arrived(sb.at[x, y, c, back_l, back_h], ps.at[k - 1], pr.at[k - 1])
    first = lambda k: ((x + (1 - c) * k) % 4, (y + c * k) % 4)
    second = lambda k: ((x + c * k) % 4, (y + (1 - c) * k) % 4)

    def core_copy(n, bx, by):
        push(lambda: sb.at[bx, by, c], lambda: sb.at[bx, by, c], es.at[n], er.at[n],
             lambda: place(x, y, zl, zh, 1 - c))

    for k in range(1, 4):
        push(lambda: sb.at[x, y, c], lambda: sb.at[x, y, c], as_.at[k - 1], ar.at[k - 1],
             lambda k=k: place(*first(k), zl, zh, c))
    order = []
    for m in range(4):
        bx, by = first(4 - m) if m else (x, y)
        if m:
            arrived(sb.at[bx, by, c], as_.at[m - 1], ar.at[m - 1])
        for k in range(1, 4):
            push(lambda bx=bx, by=by: sb.at[bx, by, c], lambda bx=bx, by=by: sb.at[bx, by, c],
                 ds.at[m, k - 1], dr.at[m, k - 1], lambda k=k: place(*second(k), zl, zh, c))
        core_copy(m, bx, by)
        order.append((bx, by))
    n = 4
    for k in range(1, 4):
        for m in range(4):
            bx, by = order[m]
            bx = (bx + c * (4 - k)) % 4
            by = (by + (1 - c) * (4 - k)) % 4
            arrived(sb.at[bx, by, c], ds.at[m, k - 1], dr.at[m, k - 1])
            core_copy(n, bx, by)
            order.append((bx, by))
            n += 1
    for n in range(16):
        m, k = n % 4, n // 4
        bx = (x + 8 - (c * m + (1 - c) * k)) % 4
        by = (y + 8 - ((1 - c) * m + c * k)) % 4
        arrived(sb.at[bx, by, 1 - c], es.at[n], er.at[n])
    for k in range(1, 4):
        other = pl.ds(((x + 4 - k) % 4) * 8, 8)
        arrived(bca.at[other], bs.at[0, k - 1], br.at[0, k - 1])
        arrived(bfa.at[other], bs.at[1, k - 1], br.at[1, k - 1])
    for when, make in sent:
        if when is None:
            make().wait_send()
        else:
            pl.when(when)(lambda make=make: make().wait_send())


def exchanged(bc, bf):
    D = pltpu.SemaphoreType.DMA
    return pl.pallas_call(
        exchange,
        out_shape=[
            jax.ShapeDtypeStruct((32, 32, 500), jnp.bfloat16),
            jax.ShapeDtypeStruct((32, 32, 512), F32),
            jax.ShapeDtypeStruct((4, 4, 2, 8, 2, 8, 256), F32),
        ],
        in_specs=[VMEM] * 2,
        out_specs=[VMEM] * 3,
        scratch_shapes=[
            pltpu.VMEM((4, 32, 500), jnp.bfloat16),
            pltpu.VMEM((4, 32, 512), F32),
            pltpu.VMEM((2, 4, 2, 2, 8, 256), F32),
            pltpu.VMEM((4, 2, 2, 8, 256), F32),
            pltpu.VMEM((4, 2, 2, 8, 256), F32),
            pltpu.VMEM((3, 2, 2, 8, 256), F32),
            pltpu.VMEM((2, 2, 8, 256), F32),
            pltpu.VMEM((2, 8, 256), F32),
            D((3, 8)), D((3, 7, 2)), D((2, 3)), D((2, 3)), D((2, 3)), D((2, 3)),
            D, D, D((3,)), D((3,)), D, D, D((15,)), D((15,)), D((3,)), D((3,)),
            D((4, 3)), D((4, 3)), D((16,)), D((16,)),
        ],
        compiler_params=pltpu.CompilerParams(collective_id=0, has_side_effects=True, vmem_limit_bytes=40 * 2**20),
        name="exchange",
    )(bc, bf)


def diagonal(w):
    sub = lax.broadcasted_iota(jnp.int32, (8, 128), 0)
    wide = (8, 128)
    for g in range(16):
        rows = slice(8 * g, 8 * g + 8)
        r0, r1 = w[rows, 0:128], w[rows, 128:256]
        cols = [jnp.broadcast_to(r0[:, 8 * g + k:8 * g + k + 1], wide) for k in range(8)]
        scale = jnp.zeros(wide, F32)
        for k in range(8):
            inv = lax.rsqrt(jnp.broadcast_to(cols[k][k:k + 1, :], wide))
            scale = jnp.where(sub == k, inv, scale)
            if k < 7:
                mult = jnp.where(sub > k, cols[k] * (inv * inv), 0.0)
                r0 = r0 - mult * jnp.broadcast_to(r0[k:k + 1, :], wide)
                r1 = r1 - mult * jnp.broadcast_to(r1[k:k + 1, :], wide)
                for j in range(k + 1, 8):
                    cols[j] = cols[j] - mult * jnp.broadcast_to(cols[j][k:k + 1, :], wide)
        u0, u1 = r0 * scale, r1 * scale
        w[rows, 0:128] = u0
        w[rows, 128:256] = u1
        if g < 15:
            change = dot(u0, jnp.concatenate([u0, u1], axis=1), 0, 0, HI)
            w[8 * g + 8:128, :] = w[8 * g + 8:128, :] - change[8 * g + 8:128, :]


def factorize(sb, s, t, w):
    row = lax.broadcasted_iota(jnp.int32, (128, 128), 0)
    col = lax.broadcasted_iota(jnp.int32, (128, 128), 1)
    eye = jnp.where(row == col, F32(1.0), F32(0.0))

    def load(zl, _):
        for a in range(4):
            for b in range(4):
                for c in range(2):
                    for h in range(2):
                        at = pl.multiple_of(b * 256 + zl * 32 + c * 16 + h * 8, 8)
                        s[pl.ds(at, 8), a * 256:a * 256 + 256] = sb[a, b, c, zl, h]
        return 0

    lax.fori_loop(0, 8, load, 0)

    def block(j, _):
        dj = pl.ds(pl.multiple_of(j * 128, 128), 128)
        w[:, 0:128] = s[dj, dj]
        w[:, 128:256] = eye
        diagonal(w)
        s[dj, dj] = jnp.where(col >= row, w[:, 0:128], 0.0)
        t[dj, :] = w[:, 128:256]

        def across(i, _):
            di = pl.ds(pl.multiple_of(i * 128, 128), 128)
            s[dj, di] = dot(t[dj, :], s[dj, di], 1, 0, HI)
            return 0

        lax.fori_loop(j + 1, 8, across, 0)

        def trailing(i, _):
            di = pl.ds(pl.multiple_of(i * 128, 128), 128)
            left = s[dj, di]

            def tile(k, _):
                dk = pl.ds(pl.multiple_of(k * 128, 128), 128)
                s[di, dk] = s[di, dk] - dot(left, s[dj, dk], 0, 0, HI)
                return 0

            lax.fori_loop(i, 8, tile, 0)
            return 0

        lax.fori_loop(j + 1, 8, trailing, 0)
        return 0

    lax.fori_loop(0, 8, block, 0)


def factorized(sb):
    return pl.pallas_call(
        factorize,
        out_shape=[jax.ShapeDtypeStruct((1024, 1024), F32), jax.ShapeDtypeStruct((1024, 128), F32)],
        in_specs=[VMEM],
        out_specs=[VMEM] * 2,
        scratch_shapes=[pltpu.VMEM((128, 256), F32)],
        compiler_params=pltpu.CompilerParams(vmem_limit_bytes=40 * 2**20),
        cost_estimate=pl.CostEstimate(flops=60 * 10**9, bytes_accessed=8 * 2**20, transcendentals=0),
        name="factorize",
    )(sb)


def finish(u, t, gu, lower, panel, r):
    d = lax.axis_index("dev")
    r[...] = gu[:, 0] * gu[:, 0] - gu[:, 1]
    for j in range(8):
        a, b = j * 128, j * 128 + 128
        xj = dot(r[:, a:b], t[a:b, :], 1, 1, HI)
        panel[0, :, a:b] = xj
        if j < 7:
            r[:, b:] = r[:, b:] - dot(xj, u[a:b, b:], 1, 0, HI)
    tile = pl.ds(pl.multiple_of((d // 4) * 128, 128), 128)
    for j in range(8):
        r2 = u[j * 128:j * 128 + 128, tile].T
        for q in range(4):
            @pl.when(d % 4 == q)
            def _(q=q):
                lower[:, j * 128:j * 128 + 128] = jnp.where(d // 4 >= j, r2[q * 32:q * 32 + 32, :], 0.0)


def finished(u, t, gu):
    return pl.pallas_call(
        finish,
        out_shape=[jax.ShapeDtypeStruct((32, 1024), F32), jax.ShapeDtypeStruct((1, 24, 1024), F32)],
        in_specs=[VMEM] * 3,
        out_specs=[VMEM] * 2,
        scratch_shapes=[pltpu.VMEM((24, 1024), F32)],
        compiler_params=pltpu.CompilerParams(vmem_limit_bytes=40 * 2**20),
        name="finish",
    )(u, t, gu)


def on_device(colloc, block_colloc, factor, block_factor):
    g = lax.axis_index("grp")
    y, zh, c = g // 4, (g // 2) % 2, g % 2
    bca, bfa, sb = exchanged(block_colloc, block_factor)
    u, t = factorized(sb)
    gram = dot(colloc, bca.reshape(1024, 500), 1, 1)
    update = dot(factor, bfa.reshape(1024, 512), 1, 1, HI)
    both = jnp.stack([gram.reshape(4, 2, 2, 24, 1024), update.reshape(4, 2, 2, 24, 1024)], axis=4)
    take = lambda v, i, ax: lax.dynamic_index_in_dim(v, i, ax, keepdims=False)
    every = range(16)
    v = take(both, c, 2) + lax.ppermute(take(both, 1 - c, 2), "grp", [(i, i ^ 1) for i in every])
    parts = [take(v, y, 0)]
    for k in range(1, 4):
        parts.append(lax.ppermute(take(v, (y + k) % 4, 0), "grp", [(i, (i + 4 * k) % 16) for i in every]))
    v = parts[0] + parts[1] + parts[2] + parts[3]
    v = take(v, zh, 0) + lax.ppermute(take(v, 1 - zh, 0), "grp", [(i, i ^ 2) for i in every])
    return tuple(finished(u, t, v))


def solution(mesh):
    placed = (P("dev", "grp"), P("dev", "grp"), P("dev", "grp"), P("dev", "grp"))
    return jax.shard_map(
        on_device,
        mesh=mesh,
        in_specs=placed,
        out_specs=(P("dev", None), P("dev", "grp", None)),
        check_vma=False,
    )
```

time: 881 us -> 251 us (0.28); the launches traced: 871 us -> 250 us
  waiting for transfers between devices: 405 us -> 22 us
  other arithmetic: 266 us -> 4.66 us
  Pallas kernels: 0 us -> 196 us
  blocking collectives: 87.9 us -> 0 us
  local copies, waits for them, and re-layouts: 46.4 us -> 5.56 us
  matrix products: 39.5 us -> 4.62 us
  between operations: 19.6 us -> 0.96 us
  starting transfers between devices: 6.57 us -> 15.9 us
    another operation x33 -> x0, other arithmetic: 258 us -> none  [the longest x30 172 us: on_device(): cholesky_factor = jnp.linalg.cholesky(schur)]
    pallas_call x0 -> x3, Pallas kernels: none -> 196 us  [the longest x1 97.2 us: factorized(): pl.pallas_call(factorize, out_shape=[jax.ShapeDtypeStruct((1024, 1024), F...]
    all_gather x1 -> x0, waiting for transfers between devices: 113 us -> none  [on_device(): schur = lax.all_gather(column_slab, 'grp', axis=1, tiled=True)]
    reduce_scatter x1 -> x0, waiting for transfers between devices: 107 us -> none  [in_one_piece(): out = lax.psum_scatter(both, axis, scatter_dimension=dim, tiled=True)]
    unnamed x4 -> x0, waiting for transfers between devices: 96 us -> none
    all_to_all x1 -> x0, waiting for transfers between devices: 89 us -> none  [copy_for_each(): return lax.all_to_all(copies, axis, split_axis=0, concat_axis=0, tiled=True)]
    all_to_all x2 -> x0, blocking collectives: 87.9 us -> none  [copy_for_each(): return lax.all_to_all(copies, axis, split_axis=0, concat_axis=0, tiled=True)]
    another operation x29 -> x0, matrix products: 33.3 us -> none  [the longest x14 23 us: on_device(): cholesky_factor = jnp.linalg.cholesky(schur)]
  transfers between devices with their start and end apart: 4 -> 5, of which waited for: 4 -> 3; matrix products, arithmetic and copies ran while one was open for 1% -> 0% of each run, Pallas kernels for 0% -> 39%
where the time goes in v1:
time: 251 us; the launch traced here: 250 us
  Pallas kernels  196 us (78%)
  waiting for transfers between devices  22 us (9%)
  starting transfers between devices  15.9 us (6%)
  local copies, waits for them, and re-layouts  5.56 us (2%)
  other arithmetic  4.66 us (2%)
  matrix products  4.62 us (2%)
    pallas_call x1, Pallas kernels, factorized(): pl.pallas_call(factorize, out_shape=[jax.ShapeDtypeStruct((1024, 1024), F...  97.2 us
    pallas_call x1, Pallas kernels, exchanged(): pl.pallas_call(exchange, out_shape=[jax.ShapeDtypeStruct((32, 32, 500), j...  93.9 us
    ppermute x3, waiting for transfers between devices, on_device(): lax.ppermute(take(v, (y + k) % 4, 0), 'grp', [(i, (i + 4 * k) % 16) for i...  18.4 us
    ppermute x3, starting transfers between devices, on_device(): lax.ppermute(take(v, (y + k) % 4, 0), 'grp', [(i, (i + 4 * k) % 16) for i...  9.31 us
    unnamed x14, local copies, waits for them, and re-layouts  5.25 us
    pallas_call x1, Pallas kernels, finished(): pl.pallas_call(finish, out_shape=[jax.ShapeDtypeStruct((32, 1024), F32),...  5.08 us
  transfers between devices with their start and end apart: 5, of which 3 were waited for; matrix products, arithmetic and copies ran while one was open for 0% of the time, Pallas kernels for 39%

profile of v1, /device:TPU:25, one launch (start us, length us, event | category | flops | bytes accessed | tf_op | source)
XLA Modules:
  0.0 249.9 jit_solution(9233192031786763247)
XLA Ops:
  0.6 0.0 copy-start
  0.7 0.0 copy-start.1
  0.7 0.9 copy-done.1
  1.6 0.0 copy-start.2
  1.6 0.8 copy-done.2
  2.3 93.9 %exchange.1 = (bf16[32,32,500]{2,1,0:T(8,128)(2,1)S(1)}, f32[32,32,512]{2,1,0:T(8,128)S(1)}, f32[4,4,2,8,2,8,256]{6,5,4,3,2,1,0:T(8,128)S(1)}) custom-call(bf16[32,500]{1,0:T(8,128)(2,1)S(1)} %copy-done.2, f32[32,512]{1,0:T(8,128)S(1)} %copy-done.1), custom_call_target="tpu_custom_call" | custom-call | tf_op jit(solution)/shard_map/exchange/pallas_call | solution.py:180
  96.2 0.0 copy-start.3
  96.3 1.9 fusion.7
  98.2 0.0 copy-done
  98.2 2.7 %fusion.8 = f32[1024,384]{0,1:T(8,128)S(1)} fusion(f32[1024,512]{1,0:T(8,128)S(1)} %bitcast.39, f32[384,512]{1,0:T(8,128)S(1)} %copy-done), kind=kOutput, calls=%fused_computation.20 | convolution fusion | flops 2415919104 | bytes 4456448 | tf_op jit(solution)/shard_map/dot_general | solution.py:18
  100.9 0.0 copy-done.3
  100.9 0.0 copy-start.5
  100.9 1.5 fusion.1
  102.4 0.2 copy-done.5
  102.6 1.9 collective-permute-start
  104.6 3.6 %collective-permute-done = f32[4,2,24,2,1024]{4,2,3,1,0:T(8,128)} collective-permute-done((f32[4,2,24,2,1024]{4,2,3,1,0:T(8,128)}, f32[4,2,24,2,1024]{4,2,3,1,0:T(8,128)}, u32[]{:S(2)}, u32[]{:S(2)}) %collective-permute-start) | collective-permute-done | bytes 1572896 | tf_op jit(solution)/shard_map/ppermute | solution.py:334
  108.3 1.9 fusion.4
  110.2 0.0 copy-start.6
  110.2 1.2 copy-done.6
  111.3 0.1 dynamic-slice_bitcast_fusion.2
  111.5 4.9 %collective-permute-start.1 = (f32[2,24,2,1024]{3,1,2,0:T(8,128)S(1)}, f32[2,24,2,1024]{3,1,2,0:T(8,128)S(1)}, u32[]{:S(2)}, u32[]{:S(2)}) collective-permute-start(f32[2,24,2,1024]{3,1,2,0:T(8,128)S(1)} %get-tuple-element.12), channel_id=1, source_target_pairs={{0,128},{32,160},{64,192},{96,224},{128,256},{160,288},{192,320},{... | collective-permute-start | bytes 1179656 | tf_op jit(solution)/shard_map/ppermute | solution.py:337
  116.3 2.5 %collective-permute-start.2 = (f32[2,24,2,1024]{3,1,2,0:T(8,128)S(1)}, f32[2,24,2,1024]{3,1,2,0:T(8,128)S(1)}, u32[]{:S(2)}, u32[]{:S(2)}) collective-permute-start(f32[2,24,2,1024]{3,1,2,0:T(8,128)S(1)} %get-tuple-element.14), channel_id=1, source_target_pairs={{0,256},{32,288},{64,320},{96,352},{128,384},{160,416},{192,448},{... | collective-permute-start | bytes 1179656 | tf_op jit(solution)/shard_map/ppermute | solution.py:337
  118.9 1.9 collective-permute-start.3
  120.8 12.1 %collective-permute-done.1 = f32[2,24,2,1024]{3,1,2,0:T(8,128)S(1)} collective-permute-done((f32[2,24,2,1024]{3,1,2,0:T(8,128)S(1)}, f32[2,24,2,1024]{3,1,2,0:T(8,128)S(1)}, u32[]{:S(2)}, u32[]{:S(2)}) %collective-permute-start.1) | collective-permute-done | bytes 393248 | tf_op jit(solution)/shard_map/ppermute | solution.py:337
  132.9 0.0 collective-permute-done.2
  132.9 6.3 %collective-permute-done.3 = f32[2,24,2,1024]{3,1,2,0:T(8,128)S(1)} collective-permute-done((f32[2,24,2,1024]{3,1,2,0:T(8,128)S(1)}, f32[2,24,2,1024]{3,1,2,0:T(8,128)S(1)}, u32[]{:S(2)}, u32[]{:S(2)}) %collective-permute-start.3) | collective-permute-done | bytes 393248 | tf_op jit(solution)/shard_map/ppermute | solution.py:337
  139.2 1.1 fusion.6
  140.3 0.2 copy.14
  140.5 4.6 %collective-permute-start.4 = (f32[24,2,1024]{2,1,0:T(2,128)S(1)}, f32[24,2,1024]{2,1,0:T(2,128)S(1)}, u32[]{:S(2)}, u32[]{:S(2)}) collective-permute-start(f32[24,2,1024]{2,1,0:T(2,128)S(1)} %bitcast.45), channel_id=1, source_target_pairs={{0,64},{32,96},{64,0},{96,32},{128,192},{160,224},{192,128},{224,1... | collective-permute-start | bytes 589832 | tf_op jit(solution)/shard_map/ppermute | solution.py:339
  145.1 0.0 copy-start.4
  145.1 2.2 copy-done.4
  147.3 97.2 %factorize.1 = (f32[1024,1024]{1,0:T(8,128)S(1)}, f32[1024,128]{1,0:T(8,128)S(1)}) custom-call(f32[4,4,2,8,2,8,256]{6,5,4,3,2,1,0:T(8,128)S(1)} %copy-done.4), custom_call_target="tpu_custom_call" | custom-call | flops 60000002048 | bytes 8388608 | tf_op jit(solution)/shard_map/factorize/pallas_call | solution.py:282
  244.5 0.0 collective-permute-done.4
  244.6 0.2 bitcast_add_fusion.1.gu
  244.8 5.1 %finish.1 = (f32[32,1024]{1,0:T(8,128)}, f32[1,24,1024]{2,1,0:T(8,128)}) custom-call(f32[1024,1024]{1,0:T(8,128)S(1)} %get-tuple-element.8.u, f32[1024,128]{1,0:T(8,128)S(1)} %get-tuple-element.9.t, f32[24,2,1024]{2,1,0:T(2,128)S(1)} %bitcast_add_fusion.1.gu), custom_call_target="tpu_custom_call" | custom-call | tf_op jit(solution)/shard_map/finish/pallas_call | solution.py:313
  (1 shorter events, 0.0 us)
Async XLA Ops:
  0.6 97.5 %copy-start = (f32[384,512]{1,0:T(8,128)S(1)}, f32[384,512]{1,0:T(8,128)}, u32[]{:S(2)}) copy-start(f32[384,512]{1,0:T(8,128)} %param.6) | copy-start | bytes 2359300
  0.7 0.9 copy-start.1
  1.6 0.8 copy-start.2
  96.2 4.7 %copy-start.3 = (f32[4,4,2,8,2,8,256]{6,5,4,3,2,1,0:T(8,128)}, f32[4,4,2,8,2,8,256]{6,5,4,3,2,1,0:T(8,128)S(1)}, u32[]{:S(2)}) copy-start(f32[4,4,2,8,2,8,256]{6,5,4,3,2,1,0:T(8,128)S(1)} %get-tuple-element.7.sb) | copy-start | bytes 12582916
  100.9 1.7 copy-start.5
  102.6 5.6 %collective-permute-start = (f32[4,2,24,2,1024]{4,2,3,1,0:T(8,128)}, f32[4,2,24,2,1024]{4,2,3,1,0:T(8,128)}, u32[]{:S(2)}, u32[]{:S(2)}) collective-permute-start(f32[4,2,24,2,1024]{4,2,3,1,0:T(8,128)} %fusion.1), channel_id=1, source_target_pairs={{0,32},{32,0},{64,96},{96,64},{128,160},{160,128},{192,224},{224,1... | collective-permute-start | bytes 4718600 | tf_op jit(solution)/shard_map/ppermute | solution.py:334
  110.2 1.2 copy-start.6
  111.5 21.5 %collective-permute-start.1 = (f32[2,24,2,1024]{3,1,2,0:T(8,128)S(1)}, f32[2,24,2,1024]{3,1,2,0:T(8,128)S(1)}, u32[]{:S(2)}, u32[]{:S(2)}) collective-permute-start(f32[2,24,2,1024]{3,1,2,0:T(8,128)S(1)} %get-tuple-element.12), channel_id=1, source_target_pairs={{0,128},{32,160},{64,192},{96,224},{128,256},{160,288},{192,320},{... | collective-permute-start | bytes 1179656 | tf_op jit(solution)/shard_map/ppermute | solution.py:337
  116.3 16.6 %collective-permute-start.2 = (f32[2,24,2,1024]{3,1,2,0:T(8,128)S(1)}, f32[2,24,2,1024]{3,1,2,0:T(8,128)S(1)}, u32[]{:S(2)}, u32[]{:S(2)}) collective-permute-start(f32[2,24,2,1024]{3,1,2,0:T(8,128)S(1)} %get-tuple-element.14), channel_id=1, source_target_pairs={{0,256},{32,288},{64,320},{96,352},{128,384},{160,416},{192,448},{... | collective-permute-start | bytes 1179656 | tf_op jit(solution)/shard_map/ppermute | solution.py:337
  118.9 20.3 %collective-permute-start.3 = (f32[2,24,2,1024]{3,1,2,0:T(8,128)S(1)}, f32[2,24,2,1024]{3,1,2,0:T(8,128)S(1)}, u32[]{:S(2)}, u32[]{:S(2)}) collective-permute-start(f32[2,24,2,1024]{3,1,2,0:T(8,128)S(1)} %get-tuple-element.13), channel_id=1, source_target_pairs={{0,384},{32,416},{64,448},{96,480},{128,0},{160,32},{192,64},{224,... | collective-permute-start | bytes 1179656 | tf_op jit(solution)/shard_map/ppermute | solution.py:337
  140.5 104.1 %collective-permute-start.4 = (f32[24,2,1024]{2,1,0:T(2,128)S(1)}, f32[24,2,1024]{2,1,0:T(2,128)S(1)}, u32[]{:S(2)}, u32[]{:S(2)}) collective-permute-start(f32[24,2,1024]{2,1,0:T(2,128)S(1)} %bitcast.45), channel_id=1, source_target_pairs={{0,64},{32,96},{64,0},{96,32},{128,192},{160,224},{192,128},{224,1... | collective-permute-start | bytes 589832 | tf_op jit(solution)/shard_map/ppermute | solution.py:339
  145.1 2.2 copy-start.4

commit v2 on v1

--- a/solution.py
+++ b/solution.py
@@ -42,11 +42,17 @@
             pl.when(when)(lambda: make().start())
         sent.append((when, make))
 
-    def arrived(ref, ssem, rsem):
-        pltpu.make_async_remote_copy(
-            src_ref=ref, dst_ref=ref, send_sem=ssem, recv_sem=rsem,
-            device_id=place(x, y, zl, zh, 1 - c), device_id_type=MESH,
-        ).wait_recv()
+    def arrived(ref, ssem, rsem, when=None):
+        def wait():
+            pltpu.make_async_remote_copy(
+                src_ref=ref, dst_ref=ref, send_sem=ssem, recv_sem=rsem,
+                device_id=place(x, y, zl, zh, 1 - c), device_id_type=MESH,
+            ).wait_recv()
+
+        if when is None:
+            wait()
+        else:
+            pl.when(when)(wait)
 
     barrier = pltpu.get_barrier_semaphore()
     ring = [(zl + k % 8) % 8 for k in range(16)]
@@ -125,28 +131,28 @@
     sb[x, y, c, zl, zh] = total[0] * total[0] + jnp.where(row == col, F32(DAMPING), F32(0.0)) - total[1]
     for k in range(1, 16):
         push(lambda: sb.at[x, y, c, zl, zh], lambda: sb.at[x, y, c, zl, zh], ps.at[k - 1], pr.at[k - 1],
-             lambda k=k: place(x, y, ring[k], half[k], c))
+             lambda k=k: place(x, y, ring[k], half[k], c), x >= y)
     for k in range(1, 16):
         back_l, back_h = (zl + 8 - k % 8) % 8, (zh + k // 8) % 2
-        arrived(sb.at[x, y, c, back_l, back_h], ps.at[k - 1], pr.at[k - 1])
+        arrived(sb.at[x, y, c, back_l, back_h], ps.at[k - 1], pr.at[k - 1], x >= y)
     first = lambda k: ((x + (1 - c) * k) % 4, (y + c * k) % 4)
     second = lambda k: ((x + c * k) % 4, (y + (1 - c) * k) % 4)
 
     def core_copy(n, bx, by):
         push(lambda: sb.at[bx, by, c], lambda: sb.at[bx, by, c], es.at[n], er.at[n],
-             lambda: place(x, y, zl, zh, 1 - c))
+             lambda: place(x, y, zl, zh, 1 - c), bx >= by)
 
     for k in range(1, 4):
         push(lambda: sb.at[x, y, c], lambda: sb.at[x, y, c], as_.at[k - 1], ar.at[k - 1],
-             lambda k=k: place(*first(k), zl, zh, c))
+             lambda k=k: place(*first(k), zl, zh, c), x >= y)
     order = []
     for m in range(4):
         bx, by = first(4 - m) if m else (x, y)
         if m:
-            arrived(sb.at[bx, by, c], as_.at[m - 1], ar.at[m - 1])
+            arrived(sb.at[bx, by, c], as_.at[m - 1], ar.at[m - 1], bx >= by)
         for k in range(1, 4):
             push(lambda bx=bx, by=by: sb.at[bx, by, c], lambda bx=bx, by=by: sb.at[bx, by, c],
-                 ds.at[m, k - 1], dr.at[m, k - 1], lambda k=k: place(*second(k), zl, zh, c))
+                 ds.at[m, k - 1], dr.at[m, k - 1], lambda k=k: place(*second(k), zl, zh, c), bx >= by)
         core_copy(m, bx, by)
         order.append((bx, by))
     n = 4
@@ -155,7 +161,7 @@
             bx, by = order[m]
             bx = (bx + c * (4 - k)) % 4
             by = (by + (1 - c) * (4 - k)) % 4
-            arrived(sb.at[bx, by, c], ds.at[m, k - 1], dr.at[m, k - 1])
+            arrived(sb.at[bx, by, c], ds.at[m, k - 1], dr.at[m, k - 1], bx >= by)
             core_copy(n, bx, by)
             order.append((bx, by))
             n += 1
@@ -163,7 +169,7 @@
         m, k = n % 4, n // 4
         bx = (x + 8 - (c * m + (1 - c) * k)) % 4
         by = (y + 8 - ((1 - c) * m + c * k)) % 4
-        arrived(sb.at[bx, by, 1 - c], es.at[n], er.at[n])
+        arrived(sb.at[bx, by, 1 - c], es.at[n], er.at[n], bx >= by)
     for k in range(1, 4):
         other = pl.ds(((x + 4 - k) % 4) * 8, 8)
         arrived(bca.at[other], bs.at[0, k - 1], br.at[0, k - 1])
@@ -199,101 +205,205 @@
             D, D, D((3,)), D((3,)), D, D, D((15,)), D((15,)), D((3,)), D((3,)),
             D((4, 3)), D((4, 3)), D((16,)), D((16,)),
         ],
-        compiler_params=pltpu.CompilerParams(collective_id=0, has_side_effects=True, vmem_limit_bytes=40 * 2**20),
+        compiler_params=pltpu.CompilerParams(collective_id=0, has_side_effects=True, vmem_limit_bytes=16 * 2**20),
         name="exchange",
     )(bc, bf)
 
 
 def diagonal(w):
-    sub = lax.broadcasted_iota(jnp.int32, (8, 128), 0)
     wide = (8, 128)
+    sub = lax.broadcasted_iota(jnp.int32, wide, 0)
+    lane = lambda v, k: jnp.broadcast_to(v[:, k:k + 1], wide)
+    line = lambda v, k: jnp.broadcast_to(v[k:k + 1, :], wide)
+    r0, r1 = w[0:8, 0:128], w[0:8, 128:256]
+    cols = [lane(r0, k) for k in range(8)]
+    pivot = line(cols[0], 0)
     for g in range(16):
-        rows = slice(8 * g, 8 * g + 8)
-        r0, r1 = w[rows, 0:128], w[rows, 128:256]
-        cols = [jnp.broadcast_to(r0[:, 8 * g + k:8 * g + k + 1], wide) for k in range(8)]
+        lo = 8 * g
+        more = g < 15
+        if more:
+            n0, n1 = w[lo + 8:lo + 16, 0:128], w[lo + 8:lo + 16, 128:256]
+            left = [lane(n0, lo + k) for k in range(8)]
+            ncols = [lane(n0, lo + 8 + k) for k in range(8)]
         scale = jnp.zeros(wide, F32)
         for k in range(8):
-            inv = lax.rsqrt(jnp.broadcast_to(cols[k][k:k + 1, :], wide))
+            inv = lax.rsqrt(pivot)
+            inv2 = inv * inv
+            if k < 7:
+                e = line(cols[k + 1], k)
+                pivot = line(cols[k + 1], k + 1) - (e * e) * inv2
+            elif more:
+                e = line(left[7], 0)
+                pivot = line(ncols[0], 0) - (e * e) * inv2
             scale = jnp.where(sub == k, inv, scale)
+            p0, p1 = line(r0, k), line(r1, k)
+            if more:
+                m2 = left[k] * inv2
             if k < 7:
-                mult = jnp.where(sub > k, cols[k] * (inv * inv), 0.0)
-                r0 = r0 - mult * jnp.broadcast_to(r0[k:k + 1, :], wide)
-                r1 = r1 - mult * jnp.broadcast_to(r1[k:k + 1, :], wide)
+                mult = jnp.where(sub > k, cols[k], 0.0) * inv2
                 for j in range(k + 1, 8):
-                    cols[j] = cols[j] - mult * jnp.broadcast_to(cols[j][k:k + 1, :], wide)
+                    e = line(cols[j], k)
+                    cols[j] = cols[j] - mult * e
+                    if more:
+                        left[j] = left[j] - m2 * e
+                r0 = r0 - mult * p0
+                r1 = r1 - mult * p1
+            if more:
+                for j in range(8):
+                    ncols[j] = ncols[j] - m2 * line(left[k], j)
+                n0 = n0 - m2 * p0
+                n1 = n1 - m2 * p1
         u0, u1 = r0 * scale, r1 * scale
-        w[rows, 0:128] = u0
-        w[rows, 128:256] = u1
-        if g < 15:
+        w[lo:lo + 8, 0:128] = u0
+        w[lo:lo + 8, 128:256] = u1
+        if g < 14:
             change = dot(u0, jnp.concatenate([u0, u1], axis=1), 0, 0, HI)
-            w[8 * g + 8:128, :] = w[8 * g + 8:128, :] - change[8 * g + 8:128, :]
-
-
-def factorize(sb, s, t, w):
+            w[lo + 16:128, :] = w[lo + 16:128, :] - change[lo + 16:128, :]
+        if more:
+            r0, r1, cols = n0, n1, ncols
+
+
+def factorize(colloc, factor, bca, bfa, sb, s, t, r, w, part, rcore, acc, ry, s2, rz, cs, cr, ys, yr, hs, hr):
+    g = lax.axis_index("grp")
+    d = lax.axis_index("dev")
+    y, zh, c = g // 4, (g // 2) % 2, g % 2
+    x, zl = d // 8, d % 8
+
+    def core_copy():
+        return pltpu.make_async_remote_copy(
+            src_ref=part.at[1 - c], dst_ref=rcore, send_sem=cs, recv_sem=cr,
+            device_id=place(x, y, zl, zh, 1 - c), device_id_type=MESH,
+        )
+
+    def y_copy(k):
+        return pltpu.make_async_remote_copy(
+            src_ref=acc.at[(y + k) % 4], dst_ref=ry.at[k - 1], send_sem=ys.at[k - 1], recv_sem=yr.at[k - 1],
+            device_id=place(x, (y + k) % 4, zl, zh, c), device_id_type=MESH,
+        )
+
+    def half_copy():
+        return pltpu.make_async_remote_copy(
+            src_ref=s2.at[1 - zh], dst_ref=rz, send_sem=hs, recv_sem=hr,
+            device_id=place(x, y, zl, 1 - zh, c), device_id_type=MESH,
+        )
+
+    barrier = pltpu.get_barrier_semaphore()
+    peers = [place(x, y, zl, zh, 1 - c), place(x, y, zl, 1 - zh, c)]
+    peers += [place(x, (y + k) % 4, zl, zh, c) for k in range(1, 4)]
+    for peer in peers:
+        pl.semaphore_signal(barrier, inc=1, device_id=peer, device_id_type=MESH)
+    for b in range(4):
+        rows = slice(96 * b, 96 * b + 96)
+        gram = dot(colloc[rows, :], bca[...], 1, 1)
+        update = dot(factor[rows, :], bfa[...], 1, 1, HI)
+        for h in range(2):
+            for k in range(2):
+                lo = (h * 2 + k) * 24
+                part[k, b, h, 0] = gram[lo:lo + 24]
+                part[k, b, h, 1] = update[lo:lo + 24]
+    pl.semaphore_wait(barrier, len(peers))
+    core_copy().start()
+
+    def load(i, _):
+        for b in range(4):
+            for k in range(2):
+                for h in range(2):
+                    at = pl.multiple_of(b * 256 + i * 32 + k * 16 + h * 8, 8)
+                    for a in range(b, 4):
+                        s[pl.ds(at, 8), a * 256:a * 256 + 256] = sb[a, b, k, i, h]
+        return 0
+
+    lax.fori_loop(0, 8, load, 0)
+
     row = lax.broadcasted_iota(jnp.int32, (128, 128), 0)
     col = lax.broadcasted_iota(jnp.int32, (128, 128), 1)
     eye = jnp.where(row == col, F32(1.0), F32(0.0))
-
-    def load(zl, _):
-        for a in range(4):
-            for b in range(4):
-                for c in range(2):
-                    for h in range(2):
-                        at = pl.multiple_of(b * 256 + zl * 32 + c * 16 + h * 8, 8)
-                        s[pl.ds(at, 8), a * 256:a * 256 + 256] = sb[a, b, c, zl, h]
-        return 0
-
-    lax.fori_loop(0, 8, load, 0)
 
     def block(j, _):
         dj = pl.ds(pl.multiple_of(j * 128, 128), 128)
         w[:, 0:128] = s[dj, dj]
         w[:, 128:256] = eye
         diagonal(w)
+        t[dj, :] = w[:, 128:256]
+
+        def across(k, _):
+            dk = pl.ds(pl.multiple_of(k * 256, 256), 256)
+            s[dj, dk] = dot(t[dj, :], s[dj, dk], 1, 0, HI)
+            return 0
+
+        lax.fori_loop((j + 1) // 2, 4, across, 0)
         s[dj, dj] = jnp.where(col >= row, w[:, 0:128], 0.0)
-        t[dj, :] = w[:, 128:256]
-
-        def across(i, _):
-            di = pl.ds(pl.multiple_of(i * 128, 128), 128)
-            s[dj, di] = dot(t[dj, :], s[dj, di], 1, 0, HI)
-            return 0
-
-        lax.fori_loop(j + 1, 8, across, 0)
 
         def trailing(i, _):
             di = pl.ds(pl.multiple_of(i * 128, 128), 128)
             left = s[dj, di]
 
             def tile(k, _):
-                dk = pl.ds(pl.multiple_of(k * 128, 128), 128)
+                dk = pl.ds(pl.multiple_of(k * 256, 256), 256)
                 s[di, dk] = s[di, dk] - dot(left, s[dj, dk], 0, 0, HI)
                 return 0
 
-            lax.fori_loop(i, 8, tile, 0)
+            lax.fori_loop(i // 2, 4, tile, 0)
             return 0
 
         lax.fori_loop(j + 1, 8, trailing, 0)
+
+        @pl.when(j == 0)
+        def _():
+            core_copy().wait_recv()
+            for b in range(4):
+                acc[b] = part[c, b] + rcore[b]
+            for k in range(1, 4):
+                y_copy(k).start()
+
+        @pl.when(j == 3)
+        def _():
+            for k in range(1, 4):
+                y_copy(k).wait_recv()
+            s2[...] = acc[y] + ry[0] + ry[1] + ry[2]
+            half_copy().start()
+
         return 0
 
     lax.fori_loop(0, 8, block, 0)
-
-
-def factorized(sb):
+    half_copy().wait_recv()
+    gram = s2[zh, 0] + rz[0]
+    r[...] = gram * gram - (s2[zh, 1] + rz[1])
+    core_copy().wait_send()
+    for k in range(1, 4):
+        y_copy(k).wait_send()
+    half_copy().wait_send()
+
+
+def factorized(colloc, factor, bca, bfa, sb):
+    D = pltpu.SemaphoreType.DMA
     return pl.pallas_call(
         factorize,
-        out_shape=[jax.ShapeDtypeStruct((1024, 1024), F32), jax.ShapeDtypeStruct((1024, 128), F32)],
-        in_specs=[VMEM],
-        out_specs=[VMEM] * 2,
-        scratch_shapes=[pltpu.VMEM((128, 256), F32)],
-        compiler_params=pltpu.CompilerParams(vmem_limit_bytes=40 * 2**20),
-        cost_estimate=pl.CostEstimate(flops=60 * 10**9, bytes_accessed=8 * 2**20, transcendentals=0),
+        out_shape=[
+            jax.ShapeDtypeStruct((1024, 1024), F32),
+            jax.ShapeDtypeStruct((1024, 128), F32),
+            jax.ShapeDtypeStruct((24, 1024), F32),
+        ],
+        in_specs=[VMEM] * 5,
+        out_specs=[VMEM] * 3,
+        scratch_shapes=[
+            pltpu.VMEM((128, 256), F32),
+            pltpu.VMEM((2, 4, 2, 2, 24, 1024), F32),
+            pltpu.VMEM((4, 2, 2, 24, 1024), F32),
+            pltpu.VMEM((4, 2, 2, 24, 1024), F32),
+            pltpu.VMEM((3, 2, 2, 24, 1024), F32),
+            pltpu.VMEM((2, 2, 24, 1024), F32),
+            pltpu.VMEM((2, 24, 1024), F32),
+            D, D, D((3,)), D((3,)), D, D,
+        ],
+        compiler_params=pltpu.CompilerParams(collective_id=1, has_side_effects=True, vmem_limit_bytes=24 * 2**20),
         name="factorize",
-    )(sb)
-
-
-def finish(u, t, gu, lower, panel, r):
+    )(colloc, factor, bca, bfa, sb)
+
+
+def finish(u, t, below, lower, panel, r):
     d = lax.axis_index("dev")
-    r[...] = gu[:, 0] * gu[:, 0] - gu[:, 1]
+    r[...] = below[...]
     for j in range(8):
         a, b = j * 128, j * 128 + 128
         xj = dot(r[:, a:b], t[a:b, :], 1, 1, HI)
@@ -309,7 +419,7 @@
                 lower[:, j * 128:j * 128 + 128] = jnp.where(d // 4 >= j, r2[q * 32:q * 32 + 32, :], 0.0)
 
 
-def finished(u, t, gu):
+def finished(u, t, below):
     return pl.pallas_call(
         finish,
         out_shape=[jax.ShapeDtypeStruct((32, 1024), F32), jax.ShapeDtypeStruct((1, 24, 1024), F32)],
@@ -318,26 +428,12 @@
         scratch_shapes=[pltpu.VMEM((24, 1024), F32)],
         compiler_params=pltpu.CompilerParams(vmem_limit_bytes=40 * 2**20),
         name="finish",
-    )(u, t, gu)
+    )(u, t, below)
 
 
 def on_device(colloc, block_colloc, factor, block_factor):
-    g = lax.axis_index("grp")
-    y, zh, c = g // 4, (g // 2) % 2, g % 2
     bca, bfa, sb = exchanged(block_colloc, block_factor)
-    u, t = factorized(sb)
-    gram = dot(colloc, bca.reshape(1024, 500), 1, 1)
-    update = dot(factor, bfa.reshape(1024, 512), 1, 1, HI)
-    both = jnp.stack([gram.reshape(4, 2, 2, 24, 1024), update.reshape(4, 2, 2, 24, 1024)], axis=4)
-    take = lambda v, i, ax: lax.dynamic_index_in_dim(v, i, ax, keepdims=False)
-    every = range(16)
-    v = take(both, c, 2) + lax.ppermute(take(both, 1 - c, 2), "grp", [(i, i ^ 1) for i in every])
-    parts = [take(v, y, 0)]
-    for k in range(1, 4):
-        parts.append(lax.ppermute(take(v, (y + k) % 4, 0), "grp", [(i, (i + 4 * k) % 16) for i in every]))
-    v = parts[0] + parts[1] + parts[2] + parts[3]
-    v = take(v, zh, 0) + lax.ppermute(take(v, 1 - zh, 0), "grp", [(i, i ^ 2) for i in every])
-    return tuple(finished(u, t, v))
+    return tuple(finished(*factorized(colloc, factor, bca.reshape(1024, 500), bfa.reshape(1024, 512), sb)))
 
 
 def solution(mesh):

time: 251 us -> 174 us (0.69)
  Pallas kernels: 196 us -> 168 us
  waiting for transfers between devices: 22 us -> 0 us
  starting transfers between devices: 15.9 us -> 0 us
  other arithmetic: 4.66 us -> 0 us
  matrix products: 4.62 us -> 0 us
    pallas_call x1, Pallas kernels: 97.2 us -> 69.3 us  [factorized(): pl.pallas_call(factorize, out_shape=[jax.ShapeDtypeStruct((1024, 1024), F...]
    ppermute x5 -> x0, waiting for transfers between devices: 22 us -> none  [the longest x3 18.4 us: on_device(): lax.ppermute(take(v, (y + k) % 4, 0), 'grp', [(i, (i + 4 * k) % 16) for i...]
    ppermute x5 -> x0, starting transfers between devices: 15.9 us -> none  [the longest x3 9.31 us: on_device(): lax.ppermute(take(v, (y + k) % 4, 0), 'grp', [(i, (i + 4 * k) % 16) for i...]
    dot_general x2 -> x0, matrix products: 4.62 us -> none  [dot(): lax.dot_general(a, b, (((ca,), (cb,)), ((), ())), precision=precision, pr...]
    add x3 -> x0, other arithmetic: 3.16 us -> none  [the longest x1 1.87 us: on_device(): take(both, c, 2)]
    unnamed x14 -> x7, local copies, waits for them, and re-layouts: 5.25 us -> 3.88 us
  transfers between devices with their start and end apart: 5 -> 0, of which waited for: 3 -> 0; matrix products, arithmetic and copies ran while one was open for 0% -> 0% of each run, Pallas kernels for 39% -> 0%
where the time goes in v2:
time: 174 us; the launch traced here: 172 us
  Pallas kernels  168 us (97%)
  local copies, waits for them, and re-layouts  3.88 us (2%)
    pallas_call x1, Pallas kernels, exchanged(): pl.pallas_call(exchange, out_shape=[jax.ShapeDtypeStruct((32, 32, 500), j...  93.4 us
    pallas_call x1, Pallas kernels, factorized(): pl.pallas_call(factorize, out_shape=[jax.ShapeDtypeStruct((1024, 1024), F...  69.3 us
    pallas_call x1, Pallas kernels, finished(): pl.pallas_call(finish, out_shape=[jax.ShapeDtypeStruct((32, 1024), F32),...  5.08 us
    unnamed x7, local copies, waits for them, and re-layouts  3.88 us

profile of v2, /device:TPU:25, one launch (start us, length us, event | category | flops | bytes accessed | tf_op | source)
XLA Modules:
  0.0 172.3 jit_solution(15428475493823265640)
XLA Ops:
  0.6 1.2 copy.6.colloc
  1.8 0.0 copy-start.1
  1.8 0.8 copy-done.1
  2.6 0.0 copy-start.2
  2.6 0.8 copy-done.2
  3.4 93.4 %exchange.1 = (bf16[32,32,500]{2,1,0:T(8,128)(2,1)S(1)}, f32[32,32,512]{2,1,0:T(8,128)S(1)}, f32[4,4,2,8,2,8,256]{6,5,4,3,2,1,0:T(8,128)S(1)}) custom-call(bf16[32,500]{1,0:T(8,128)(2,1)S(1)} %copy-done.2, f32[32,512]{1,0:T(8,128)S(1)} %copy-done.1), custom_call_target="tpu_custom_call" | custom-call | tf_op jit(solution)/shard_map/exchange/pallas_call | solution.py:186
  96.8 0.0 copy-start
  96.8 1.1 copy-done
  97.9 69.3 %factorize.1 = (f32[1024,1024]{1,0:T(8,128)S(1)}, f32[1024,128]{1,0:T(8,128)S(1)}, f32[24,1024]{1,0:T(8,128)S(1)}) custom-call(bf16[384,500]{1,0:T(8,128)(2,1)S(1)} %copy.6.colloc, f32[384,512]{1,0:T(8,128)S(1)} %copy-done, bf16[1024,500]{1,0:T(8,128)(2,1)S(1)} %bitcast.3, f32[1024,512]{1,0:T(8,128)S(1)} %bitcast.2, ...), custom_call_target="tpu_custom_call" | custom-call | tf_op jit(solution)/shard_map/factorize/pallas_call | solution.py:380
  167.3 5.1 %finish.1 = (f32[32,1024]{1,0:T(8,128)}, f32[1,24,1024]{2,1,0:T(8,128)}) custom-call(f32[1024,1024]{1,0:T(8,128)S(1)} %get-tuple-element.11.u, f32[1024,128]{1,0:T(8,128)S(1)} %get-tuple-element.12.t, f32[24,1024]{1,0:T(8,128)S(1)} %get-tuple-element.13.below), custom_call_target="tpu_custom_call" | custom-call | tf_op jit(solution)/shard_map/finish/pallas_call | solution.py:423
Async XLA Ops:
  1.8 0.8 copy-start.1
  2.6 0.8 copy-start.2
  96.8 1.1 copy-start

commit v3 on v2

--- a/solution.py
+++ b/solution.py
@@ -22,13 +22,22 @@
     return {"grp": y * 4 + zh * 2 + c, "dev": x * 8 + zl}
 
 
-def exchange(bc, bf, bca, bfa, sb, xbc, xbf, part, rcore, acc, ry, s2, rz,
-             zr, zs, xr, xs, br, bs, cr, cs, yr, ys, hr, hs, pr, ps, ar, as_, dr, ds, er, es):
+def exchange(colloc, bc, factor, bf, acc, sb, bca, bfa, tall, wide, part, theirs, dpart, rcore, dacc, ry, s2, rz,
+             ls, zr, zs, xr, xs, cs, cr, ys, yr, hs, hr, pr, ps, ar, as_, dr, ds, gr, gs, er, es, fs, fr):
     g = lax.axis_index("grp")
     d = lax.axis_index("dev")
     y, zh, c = g // 4, (g // 2) % 2, g % 2
     x, zl = d // 8, d % 8
     sent = []
+
+    local = [
+        pltpu.make_async_copy(bc, bca.at[d], ls.at[0]),
+        pltpu.make_async_copy(bf, bfa.at[d], ls.at[1]),
+        pltpu.make_async_copy(colloc, tall, ls.at[2]),
+        pltpu.make_async_copy(factor, wide, ls.at[3]),
+    ]
+    for copy in local:
+        copy.start()
 
     def push(src, dst, ssem, rsem, to, when=None):
         def make():
@@ -70,19 +79,33 @@
         (bf.at[0:16], lambda slot: bfa.at[slot, 0:16]),
         (bf.at[16:32], lambda slot: bfa.at[slot, 16:32]),
     ]
+    whole = [(bc, lambda slot: bca.at[slot]), (bf, lambda slot: bfa.at[slot])]
+    over = [lambda: place((x + 1) % 4, y, zl, zh, c), lambda: place((x + 3) % 4, y, zl, zh, c)]
+
+    def to_x(src, own, when=None):
+        for q, (mine, at) in enumerate(whole):
+            for way in range(2):
+                source = (lambda mine=mine: mine) if own else (lambda at=at: at(x * 8 + src))
+                push(source, lambda at=at: at(x * 8 + src), xs.at[way, q, src], xr.at[way, q, src], over[way], when)
+
+    def from_x(src):
+        for q, (_, at) in enumerate(whole):
+            for way in range(2):
+                slot = ((x + 3 + 2 * way) % 4) * 8 + src
+                arrived(at(slot), xs.at[way, q, src], xr.at[way, q, src])
+                push(lambda at=at, slot=slot: at(slot), lambda at=at, slot=slot: at(slot),
+                     xs.at[2, q, src], xr.at[2, q, src], over[way], (src % 2) == way)
+
+    def from_far(src):
+        for q, (_, at) in enumerate(whole):
+            arrived(at(((x + 2) % 4) * 8 + src), xs.at[2, q, src], xr.at[2, q, src])
+
     for q, (own, at) in enumerate(chunks):
         for way, step in ((0, 1), (1, -1)):
             ok = (zl < 7) if step == 1 else (zl > 0)
             push(lambda own=own: own, lambda at=at: at(d), zs.at[q, 0, way], zr.at[q, zl],
                  lambda step=step: place(x, y, zl + step, zh, c), ok)
-    for k in range(1, 4):
-        to = lambda k=k: place((x + k) % 4, y, zl, zh, c)
-        push(lambda: bc, lambda: xbc.at[x], xs.at[0, k - 1], xr.at[0, k - 1], to)
-        push(lambda: bf, lambda: xbf.at[x], xs.at[1, k - 1], xr.at[1, k - 1], to)
-    bca[d] = bc[...]
-    bfa[d] = bf[...]
-    xbc[x] = bc[...]
-    xbf[x] = bf[...]
+    to_x(zl, True)
     for s in range(1, 8):
         for q, (own, at) in enumerate(chunks):
             for way, step in ((0, 1), (1, -1)):
@@ -98,32 +121,53 @@
                     push(lambda at=at, src=src: at(x * 8 + src), lambda at=at, src=src: at(x * 8 + src),
                          zs.at[q, s, way], zr.at[q, src],
                          lambda step=step: place(x, y, zl + step, zh, c), jnp.logical_and(inside, more))
+        for step in (1, -1):
+            src = zl - step * s
+            to_x(src, False, (src >= 0) if step == 1 else (src <= 7))
+        if s == 2:
+            from_x(zl)
     mine = pl.ds(x * 8, 8)
-    for k in range(1, 4):
-        to = lambda k=k: place((x + k) % 4, y, zl, zh, c)
-        push(lambda: bca.at[mine], lambda: bca.at[mine], bs.at[0, k - 1], br.at[0, k - 1], to)
-        push(lambda: bfa.at[mine], lambda: bfa.at[mine], bs.at[1, k - 1], br.at[1, k - 1], to)
-    for k in range(1, 4):
-        arrived(xbc.at[(x + 4 - k) % 4], xs.at[0, k - 1], xr.at[0, k - 1])
-        arrived(xbf.at[(x + 4 - k) % 4], xs.at[1, k - 1], xr.at[1, k - 1])
-    gram = dot(xbc[...].reshape(128, 500), bca[mine].reshape(256, 500), 1, 1)
-    update = dot(xbf[...].reshape(128, 512), bfa[mine].reshape(256, 512), 1, 1, HI)
+    local[0].wait()
+    local[1].wait()
+    from_far(zl)
+    rows = [a * 8 + zl for a in range(4)]
+    gram = dot(jnp.concatenate([bca[i] for i in rows], axis=0), bca[mine].reshape(256, 500), 1, 1)
+    update = dot(jnp.concatenate([bfa[i] for i in rows], axis=0), bfa[mine].reshape(256, 512), 1, 1, HI)
     for a in range(4):
         for b in range(2):
             for e in range(2):
                 lo = a * 32 + b * 16 + e * 8
-                part[b, a, e, 0] = gram[lo:lo + 8]
-                part[b, a, e, 1] = update[lo:lo + 8]
-    push(lambda: part.at[1 - c], lambda: rcore, cs, cr, lambda: place(x, y, zl, zh, 1 - c))
+                dpart[b, a, e, 0] = gram[lo:lo + 8]
+                dpart[b, a, e, 1] = update[lo:lo + 8]
+    push(lambda: dpart.at[1 - c], lambda: rcore, cs, cr, lambda: place(x, y, zl, zh, 1 - c))
+    for k in range(1, 8):
+        from_x((zl + k) % 8)
     arrived(rcore, cs, cr)
-    acc[...] = part[c] + rcore[...]
+    dacc[...] = dpart[c] + rcore[...]
     for k in range(1, 4):
-        push(lambda k=k: acc.at[(y + k) % 4], lambda k=k: ry.at[k - 1], ys.at[k - 1], yr.at[k - 1],
+        push(lambda k=k: dacc.at[(y + k) % 4], lambda k=k: ry.at[k - 1], ys.at[k - 1], yr.at[k - 1],
              lambda k=k: place(x, (y + k) % 4, zl, zh, c))
     for k in range(1, 4):
         arrived(ry.at[k - 1], ys.at[k - 1], yr.at[k - 1])
-    s2[...] = acc[y] + ry[0] + ry[1] + ry[2]
+    s2[...] = dacc[y] + ry[0] + ry[1] + ry[2]
     push(lambda: s2.at[1 - zh], lambda: rz, hs, hr, lambda: place(x, y, zl, 1 - zh, c))
+    for k in range(1, 8):
+        from_far((zl + k) % 8)
+    local[2].wait()
+    local[3].wait()
+    for b in range(3):
+        gram = dot(tall[:, 128 * b:128 * b + 128], bca[...].reshape(1024, 500), 0, 1)
+        for n in range(16):
+            lo, hi = max(24 * n, 128 * b), min(24 * n + 24, 128 * b + 128)
+            if lo < hi:
+                part[n % 2, n // 4, (n // 2) % 2, 0, lo - 24 * n:hi - 24 * n] = gram[lo - 128 * b:hi - 128 * b]
+    for b in range(4):
+        update = dot(wide[96 * b:96 * b + 96, :], bfa[...].reshape(1024, 512), 1, 1, HI)
+        for h in range(2):
+            for k in range(2):
+                lo = (h * 2 + k) * 24
+                part[k, b, h, 1] = update[lo:lo + 24]
+    push(lambda: part.at[1 - c], lambda: theirs, fs, fr, lambda: place(x, y, zl, zh, 1 - c))
     arrived(rz, hs, hr)
     total = s2[zh] + rz[...]
     row = y * 256 + zl * 32 + c * 16 + zh * 8 + lax.broadcasted_iota(jnp.int32, (8, 256), 0)
@@ -146,34 +190,37 @@
         push(lambda: sb.at[x, y, c], lambda: sb.at[x, y, c], as_.at[k - 1], ar.at[k - 1],
              lambda k=k: place(*first(k), zl, zh, c), x >= y)
     order = []
+    beside = [lambda: place(*second(1), zl, zh, c), lambda: place(*second(3), zl, zh, c)]
     for m in range(4):
         bx, by = first(4 - m) if m else (x, y)
         if m:
             arrived(sb.at[bx, by, c], as_.at[m - 1], ar.at[m - 1], bx >= by)
-        for k in range(1, 4):
+        for way in range(2):
             push(lambda bx=bx, by=by: sb.at[bx, by, c], lambda bx=bx, by=by: sb.at[bx, by, c],
-                 ds.at[m, k - 1], dr.at[m, k - 1], lambda k=k: place(*second(k), zl, zh, c), bx >= by)
+                 ds.at[m, way], dr.at[m, way], beside[way], bx >= by)
         core_copy(m, bx, by)
         order.append((bx, by))
-    n = 4
-    for k in range(1, 4):
-        for m in range(4):
-            bx, by = order[m]
-            bx = (bx + c * (4 - k)) % 4
-            by = (by + (1 - c) * (4 - k)) % 4
-            arrived(sb.at[bx, by, c], ds.at[m, k - 1], dr.at[m, k - 1], bx >= by)
-            core_copy(n, bx, by)
-            order.append((bx, by))
-            n += 1
+    shifted = lambda m, k: ((order[m][0] + c * k) % 4, (order[m][1] + (1 - c) * k) % 4)
+    for m in range(4):
+        for way in range(2):
+            bx, by = shifted(m, 3 - 2 * way)
+            arrived(sb.at[bx, by, c], ds.at[m, way], dr.at[m, way], bx >= by)
+            part_of = lambda bx=bx, by=by, way=way: sb.at[bx, by, c, way * 4:way * 4 + 4]
+            push(part_of, part_of, gs.at[m, way], gr.at[m, way], beside[way], bx >= by)
+            core_copy(4 + (8 * way) + m, bx, by)
+    arrived(theirs, fs, fr)
+    for b in range(4):
+        acc[b] = part[c, b] + theirs[b]
+    for m in range(4):
+        bx, by = shifted(m, 2)
+        for way in range(2):
+            arrived(sb.at[bx, by, c, way * 4:way * 4 + 4], gs.at[m, way], gr.at[m, way], bx >= by)
+        core_copy(8 + m, bx, by)
     for n in range(16):
         m, k = n % 4, n // 4
         bx = (x + 8 - (c * m + (1 - c) * k)) % 4
         by = (y + 8 - ((1 - c) * m + c * k)) % 4
         arrived(sb.at[bx, by, 1 - c], es.at[n], er.at[n], bx >= by)
-    for k in range(1, 4):
-        other = pl.ds(((x + 4 - k) % 4) * 8, 8)
-        arrived(bca.at[other], bs.at[0, k - 1], br.at[0, k - 1])
-        arrived(bfa.at[other], bs.at[1, k - 1], br.at[1, k - 1])
     for when, make in sent:
         if when is None:
             make().wait_send()
@@ -181,33 +228,37 @@
             pl.when(when)(lambda make=make: make().wait_send())
 
 
-def exchanged(bc, bf):
+def exchanged(colloc, bc, factor, bf):
     D = pltpu.SemaphoreType.DMA
+    whole = pl.BlockSpec(memory_space=pltpu.MemorySpace.HBM)
     return pl.pallas_call(
         exchange,
         out_shape=[
-            jax.ShapeDtypeStruct((32, 32, 500), jnp.bfloat16),
-            jax.ShapeDtypeStruct((32, 32, 512), F32),
+            jax.ShapeDtypeStruct((4, 2, 2, 24, 1024), F32),
             jax.ShapeDtypeStruct((4, 4, 2, 8, 2, 8, 256), F32),
         ],
-        in_specs=[VMEM] * 2,
-        out_specs=[VMEM] * 3,
+        in_specs=[whole] * 4,
+        out_specs=[VMEM] * 2,
         scratch_shapes=[
-            pltpu.VMEM((4, 32, 500), jnp.bfloat16),
-            pltpu.VMEM((4, 32, 512), F32),
+            pltpu.VMEM((32, 32, 500), jnp.bfloat16),
+            pltpu.VMEM((32, 32, 512), F32),
+            pltpu.VMEM((500, 384), jnp.bfloat16),
+            pltpu.VMEM((384, 512), F32),
+            pltpu.VMEM((2, 4, 2, 2, 24, 1024), F32),
+            pltpu.VMEM((4, 2, 2, 24, 1024), F32),
             pltpu.VMEM((2, 4, 2, 2, 8, 256), F32),
             pltpu.VMEM((4, 2, 2, 8, 256), F32),
             pltpu.VMEM((4, 2, 2, 8, 256), F32),
             pltpu.VMEM((3, 2, 2, 8, 256), F32),
             pltpu.VMEM((2, 2, 8, 256), F32),
             pltpu.VMEM((2, 8, 256), F32),
-            D((3, 8)), D((3, 7, 2)), D((2, 3)), D((2, 3)), D((2, 3)), D((2, 3)),
+            D((4,)), D((3, 8)), D((3, 7, 2)), D((3, 2, 8)), D((3, 2, 8)),
             D, D, D((3,)), D((3,)), D, D, D((15,)), D((15,)), D((3,)), D((3,)),
-            D((4, 3)), D((4, 3)), D((16,)), D((16,)),
+            D((4, 2)), D((4, 2)), D((4, 2)), D((4, 2)), D((16,)), D((16,)), D, D,
         ],
-        compiler_params=pltpu.CompilerParams(collective_id=0, has_side_effects=True, vmem_limit_bytes=16 * 2**20),
+        compiler_params=pltpu.CompilerParams(collective_id=0, has_side_effects=True, vmem_limit_bytes=30 * 2**20),
         name="exchange",
-    )(bc, bf)
+    )(colloc, bc, factor, bf)
 
 
 def diagonal(w):
@@ -257,23 +308,26 @@
         w[lo:lo + 8, 0:128] = u0
         w[lo:lo + 8, 128:256] = u1
         if g < 14:
-            change = dot(u0, jnp.concatenate([u0, u1], axis=1), 0, 0, HI)
-            w[lo + 16:128, :] = w[lo + 16:128, :] - change[lo + 16:128, :]
+            flipped = u0.T
+            q0 = [line(u0, k) for k in range(8)]
+            q1 = [line(u1, k) for k in range(8)]
+            for h in range(8 * g + 16, 128, 8):
+                a0, a1 = w[h:h + 8, 0:128], w[h:h + 8, 128:256]
+                for k in range(8):
+                    m = jnp.broadcast_to(flipped[h:h + 8, k:k + 1], wide)
+                    a0 = a0 - m * q0[k]
+                    a1 = a1 - m * q1[k]
+                w[h:h + 8, 0:128] = a0
+                w[h:h + 8, 128:256] = a1
         if more:
             r0, r1, cols = n0, n1, ncols
 
 
-def factorize(colloc, factor, bca, bfa, sb, s, t, r, w, part, rcore, acc, ry, s2, rz, cs, cr, ys, yr, hs, hr):
+def factorize(acc, sb, s, t, r, w, ry, s2, rz, ys, yr, hs, hr):
     g = lax.axis_index("grp")
     d = lax.axis_index("dev")
     y, zh, c = g // 4, (g // 2) % 2, g % 2
     x, zl = d // 8, d % 8
-
-    def core_copy():
-        return pltpu.make_async_remote_copy(
-            src_ref=part.at[1 - c], dst_ref=rcore, send_sem=cs, recv_sem=cr,
-            device_id=place(x, y, zl, zh, 1 - c), device_id_type=MESH,
-        )
 
     def y_copy(k):
         return pltpu.make_async_remote_copy(
@@ -288,21 +342,10 @@
         )
 
     barrier = pltpu.get_barrier_semaphore()
-    peers = [place(x, y, zl, zh, 1 - c), place(x, y, zl, 1 - zh, c)]
+    peers = [place(x, y, zl, 1 - zh, c)]
     peers += [place(x, (y + k) % 4, zl, zh, c) for k in range(1, 4)]
     for peer in peers:
         pl.semaphore_signal(barrier, inc=1, device_id=peer, device_id_type=MESH)
-    for b in range(4):
-        rows = slice(96 * b, 96 * b + 96)
-        gram = dot(colloc[rows, :], bca[...], 1, 1)
-        update = dot(factor[rows, :], bfa[...], 1, 1, HI)
-        for h in range(2):
-            for k in range(2):
-                lo = (h * 2 + k) * 24
-                part[k, b, h, 0] = gram[lo:lo + 24]
-                part[k, b, h, 1] = update[lo:lo + 24]
-    pl.semaphore_wait(barrier, len(peers))
-    core_copy().start()
 
     def load(i, _):
         for b in range(4):
@@ -314,6 +357,9 @@
         return 0
 
     lax.fori_loop(0, 8, load, 0)
+    pl.semaphore_wait(barrier, len(peers))
+    for k in range(1, 4):
+        y_copy(k).start()
 
     row = lax.broadcasted_iota(jnp.int32, (128, 128), 0)
     col = lax.broadcasted_iota(jnp.int32, (128, 128), 1)
@@ -348,14 +394,6 @@
 
         lax.fori_loop(j + 1, 8, trailing, 0)
 
-        @pl.when(j == 0)
-        def _():
-            core_copy().wait_recv()
-            for b in range(4):
-                acc[b] = part[c, b] + rcore[b]
-            for k in range(1, 4):
-                y_copy(k).start()
-
         @pl.when(j == 3)
         def _():
             for k in range(1, 4):
@@ -369,13 +407,12 @@
     half_copy().wait_recv()
     gram = s2[zh, 0] + rz[0]
     r[...] = gram * gram - (s2[zh, 1] + rz[1])
-    core_copy().wait_send()
     for k in range(1, 4):
         y_copy(k).wait_send()
     half_copy().wait_send()
 
 
-def factorized(colloc, factor, bca, bfa, sb):
+def factorized(acc, sb):
     D = pltpu.SemaphoreType.DMA
     return pl.pallas_call(
         factorize,
@@ -384,21 +421,18 @@
             jax.ShapeDtypeStruct((1024, 128), F32),
             jax.ShapeDtypeStruct((24, 1024), F32),
         ],
-        in_specs=[VMEM] * 5,
+        in_specs=[VMEM] * 2,
         out_specs=[VMEM] * 3,
         scratch_shapes=[
             pltpu.VMEM((128, 256), F32),
-            pltpu.VMEM((2, 4, 2, 2, 24, 1024), F32),
-            pltpu.VMEM((4, 2, 2, 24, 1024), F32),
-            pltpu.VMEM((4, 2, 2, 24, 1024), F32),
             pltpu.VMEM((3, 2, 2, 24, 1024), F32),
             pltpu.VMEM((2, 2, 24, 1024), F32),
             pltpu.VMEM((2, 24, 1024), F32),
-            D, D, D((3,)), D((3,)), D, D,
+            D((3,)), D((3,)), D, D,
         ],
         compiler_params=pltpu.CompilerParams(collective_id=1, has_side_effects=True, vmem_limit_bytes=24 * 2**20),
         name="factorize",
-    )(colloc, factor, bca, bfa, sb)
+    )(acc, sb)
 
 
 def finish(u, t, below, lower, panel, r):
@@ -432,8 +466,8 @@
 
 
 def on_device(colloc, block_colloc, factor, block_factor):
-    bca, bfa, sb = exchanged(block_colloc, block_factor)
-    return tuple(finished(*factorized(colloc, factor, bca.reshape(1024, 500), bfa.reshape(1024, 512), sb)))
+    acc, sb = exchanged(colloc.T, block_colloc, factor, block_factor)
+    return tuple(finished(*factorized(acc, sb)))
 
 
 def solution(mesh):

time: 174 us -> 160 us (0.920)
  Pallas kernels: 168 us -> 155 us
    pallas_call x1, Pallas kernels: 93.4 us -> 86.5 us  [exchanged(): pl.pallas_call(exchange, out_shape=[jax.ShapeDtypeStruct((4, 2, 2, 24, 10...]
    pallas_call x1, Pallas kernels: 69.3 us -> 63.7 us  [factorized(): pl.pallas_call(factorize, out_shape=[jax.ShapeDtypeStruct((1024, 1024), F...]
    unnamed x7 -> x8, local copies, waits for them, and re-layouts: 3.88 us -> 3.72 us
where the time goes in v3:
time: 160 us
  Pallas kernels  155 us (97%)
  local copies, waits for them, and re-layouts  3.72 us (2%)
    pallas_call x1, Pallas kernels, exchanged(): pl.pallas_call(exchange, out_shape=[jax.ShapeDtypeStruct((4, 2, 2, 24, 10...  86.5 us
    pallas_call x1, Pallas kernels, factorized(): pl.pallas_call(factorize, out_shape=[jax.ShapeDtypeStruct((1024, 1024), F...  63.7 us
    pallas_call x1, Pallas kernels, finished(): pl.pallas_call(finish, out_shape=[jax.ShapeDtypeStruct((32, 1024), F32),...  5.08 us
    unnamed x8, local copies, waits for them, and re-layouts  3.72 us

profile of v3, /device:TPU:25, one launch (start us, length us, event | category | flops | bytes accessed | tf_op | source)
XLA Modules:
  0.0 159.6 jit_solution(5042091319982728846)
XLA Ops:
  0.6 0.0 copy-start
  0.6 1.1 copy-done
  1.8 0.0 copy-start.1
  1.8 1.0 copy-done.1
  2.8 0.0 copy-start.2
  2.8 0.8 copy-done.2
  3.6 0.0 copy-start.3
  3.6 0.8 copy-done.3
  4.4 86.5 %exchange.1 = (f32[4,2,2,24,1024]{4,3,2,1,0:T(8,128)S(1)}, f32[4,4,2,8,2,8,256]{6,5,4,3,2,1,0:T(8,128)S(1)}) custom-call(bf16[500,384]{1,0:T(8,128)(2,1)S(1)} %bitcast.1, bf16[32,500]{1,0:T(8,128)(2,1)S(1)} %copy-done.3, f32[384,512]{1,0:T(8,128)S(1)} %copy-done, f32[32,512]{1,0:T(8,128)S(1)} %copy-done.2), custom_call_target="tpu_custom_call" | custom-call | tf_op jit(solution)/shard_map/exchange/pallas_call | solution.py:234
  90.9 63.7 %factorize.1 = (f32[1024,1024]{1,0:T(8,128)S(1)}, f32[1024,128]{1,0:T(8,128)S(1)}, f32[24,1024]{1,0:T(8,128)S(1)}) custom-call(f32[4,2,2,24,1024]{4,3,2,1,0:T(8,128)S(1)} %get-tuple-element.7.acc, f32[4,4,2,8,2,8,256]{6,5,4,3,2,1,0:T(8,128)S(1)} %get-tuple-element.8.sb), custom_call_target="tpu_custom_call" | custom-call | tf_op jit(solution)/shard_map/factorize/pallas_call | solution.py:417
  154.5 5.1 %finish.1 = (f32[32,1024]{1,0:T(8,128)}, f32[1,24,1024]{2,1,0:T(8,128)}) custom-call(f32[1024,1024]{1,0:T(8,128)S(1)} %get-tuple-element.9.u, f32[1024,128]{1,0:T(8,128)S(1)} %get-tuple-element.10.t, f32[24,1024]{1,0:T(8,128)S(1)} %get-tuple-element.11.below), custom_call_target="tpu_custom_call" | custom-call | tf_op jit(solution)/shard_map/finish/pallas_call | solution.py:457
Async XLA Ops:
  0.6 1.1 copy-start
  1.8 1.0 copy-start.1
  2.8 0.8 copy-start.2
  3.6 0.8 copy-start.3

commit v4 on v3

--- a/solution.py
+++ b/solution.py
@@ -307,11 +307,13 @@
         u0, u1 = r0 * scale, r1 * scale
         w[lo:lo + 8, 0:128] = u0
         w[lo:lo + 8, 128:256] = u1
-        if g < 14:
+        first = g // 4 * 4
+        reach = min(16, first + 6)
+        if g + 2 < reach:
             flipped = u0.T
             q0 = [line(u0, k) for k in range(8)]
             q1 = [line(u1, k) for k in range(8)]
-            for h in range(8 * g + 16, 128, 8):
+            for h in range(8 * g + 16, 8 * reach, 8):
                 a0, a1 = w[h:h + 8, 0:128], w[h:h + 8, 128:256]
                 for k in range(8):
                     m = jnp.broadcast_to(flipped[h:h + 8, k:k + 1], wide)
@@ -319,6 +321,10 @@
                     a1 = a1 - m * q1[k]
                 w[h:h + 8, 0:128] = a0
                 w[h:h + 8, 128:256] = a1
+        if g == first + 3 and reach < 16:
+            panel = w[8 * first:8 * first + 32, :]
+            change = dot(panel[:, 0:128], panel, 0, 0, HI)
+            w[8 * reach:128, :] = w[8 * reach:128, :] - change[8 * reach:128, :]
         if more:
             r0, r1, cols = n0, n1, ncols
 
@@ -380,19 +386,25 @@
         lax.fori_loop((j + 1) // 2, 4, across, 0)
         s[dj, dj] = jnp.where(col >= row, w[:, 0:128], 0.0)
 
-        def trailing(i, _):
-            di = pl.ds(pl.multiple_of(i * 128, 128), 128)
-            left = s[dj, di]
+        def update(rows, start):
+            left = s[dj, rows]
 
             def tile(k, _):
                 dk = pl.ds(pl.multiple_of(k * 256, 256), 256)
-                s[di, dk] = s[di, dk] - dot(left, s[dj, dk], 0, 0, HI)
+                s[rows, dk] = s[rows, dk] - dot(left, s[dj, dk], 0, 0, HI)
                 return 0
 
-            lax.fori_loop(i // 2, 4, tile, 0)
+            lax.fori_loop(start, 4, tile, 0)
+
+        @pl.when(j % 2 == 0)
+        def _():
+            update(pl.ds(pl.multiple_of(jnp.minimum(j + 1, 7) * 128, 128), 128), j // 2)
+
+        def trailing(i, _):
+            update(pl.ds(pl.multiple_of(i * 256, 256), 256), i)
             return 0
 
-        lax.fori_loop(j + 1, 8, trailing, 0)
+        lax.fori_loop(j // 2 + 1, 4, trailing, 0)
 
         @pl.when(j == 3)
         def _():

time: 160 us -> 152 us (0.950)
  Pallas kernels: 155 us -> 148 us
    pallas_call x1, Pallas kernels: 63.7 us -> 56 us  [factorized(): pl.pallas_call(factorize, out_shape=[jax.ShapeDtypeStruct((1024, 1024), F...]
where the time goes in v4:
time: 152 us
  Pallas kernels  148 us (97%)
  local copies, waits for them, and re-layouts  3.72 us (2%)
    pallas_call x1, Pallas kernels, exchanged(): pl.pallas_call(exchange, out_shape=[jax.ShapeDtypeStruct((4, 2, 2, 24, 10...  86.5 us
    pallas_call x1, Pallas kernels, factorized(): pl.pallas_call(factorize, out_shape=[jax.ShapeDtypeStruct((1024, 1024), F...  56 us
    pallas_call x1, Pallas kernels, finished(): pl.pallas_call(finish, out_shape=[jax.ShapeDtypeStruct((32, 1024), F32),...  5.08 us
    unnamed x8, local copies, waits for them, and re-layouts  3.72 us

profile of v4, /device:TPU:25, one launch (start us, length us, event | category | flops | bytes accessed | tf_op | source)
XLA Modules:
  0.0 151.9 jit_solution(12942276913796299425)
XLA Ops:
  0.6 0.0 copy-start
  0.6 1.1 copy-done
  1.8 0.0 copy-start.1
  1.8 1.0 copy-done.1
  2.8 0.0 copy-start.2
  2.8 0.8 copy-done.2
  3.6 0.0 copy-start.3
  3.6 0.8 copy-done.3
  4.4 86.5 %exchange.1 = (f32[4,2,2,24,1024]{4,3,2,1,0:T(8,128)S(1)}, f32[4,4,2,8,2,8,256]{6,5,4,3,2,1,0:T(8,128)S(1)}) custom-call(bf16[500,384]{1,0:T(8,128)(2,1)S(1)} %bitcast.1, bf16[32,500]{1,0:T(8,128)(2,1)S(1)} %copy-done.3, f32[384,512]{1,0:T(8,128)S(1)} %copy-done, f32[32,512]{1,0:T(8,128)S(1)} %copy-done.2), custom_call_target="tpu_custom_call" | custom-call | tf_op jit(solution)/shard_map/exchange/pallas_call | solution.py:234
  90.9 56.0 %factorize.1 = (f32[1024,1024]{1,0:T(8,128)S(1)}, f32[1024,128]{1,0:T(8,128)S(1)}, f32[24,1024]{1,0:T(8,128)S(1)}) custom-call(f32[4,2,2,24,1024]{4,3,2,1,0:T(8,128)S(1)} %get-tuple-element.7.acc, f32[4,4,2,8,2,8,256]{6,5,4,3,2,1,0:T(8,128)S(1)} %get-tuple-element.8.sb), custom_call_target="tpu_custom_call" | custom-call | tf_op jit(solution)/shard_map/factorize/pallas_call | solution.py:429
  146.8 5.1 %finish.1 = (f32[32,1024]{1,0:T(8,128)}, f32[1,24,1024]{2,1,0:T(8,128)}) custom-call(f32[1024,1024]{1,0:T(8,128)S(1)} %get-tuple-element.9.u, f32[1024,128]{1,0:T(8,128)S(1)} %get-tuple-element.10.t, f32[24,1024]{1,0:T(8,128)S(1)} %get-tuple-element.11.below), custom_call_target="tpu_custom_call" | custom-call | tf_op jit(solution)/shard_map/finish/pallas_call | solution.py:469
Async XLA Ops:
  0.6 1.1 copy-start
  1.8 1.0 copy-start.1
  2.8 0.8 copy-start.2
  3.6 0.8 copy-start.3

commit v5 on v4

v5 whole, which is shorter than its diff:
```python
import functools

import jax
import jax.numpy as jnp
from jax import lax
from jax.experimental import pallas as pl
from jax.experimental.pallas import tpu as pltpu
from jax.sharding import PartitionSpec as P

DAMPING = 0.0625
HI = lax.Precision.HIGHEST
MESH = pl.DeviceIdType.MESH
F32 = jnp.float32
VMEM = pl.BlockSpec(memory_space=pltpu.VMEM)


def dot(a, b, ca, cb, precision=None):
    return lax.dot_general(a, b, (((ca,), (cb,)), ((), ())), precision=precision, preferred_element_type=F32)


def place(x, y, zl, zh, c):
    return {"grp": y * 4 + zh * 2 + c, "dev": x * 8 + zl}


def diagonal(w):
    wide = (8, 128)
    sub = lax.broadcasted_iota(jnp.int32, wide, 0)
    lane = lambda v, k: jnp.broadcast_to(v[:, k:k + 1], wide)
    line = lambda v, k: jnp.broadcast_to(v[k:k + 1, :], wide)
    r0, r1 = w[0:8, 0:128], w[0:8, 128:256]
    cols = [lane(r0, k) for k in range(8)]
    pivot = line(cols[0], 0)
    for g in range(16):
        lo = 8 * g
        more = g < 15
        if more:
            n0, n1 = w[lo + 8:lo + 16, 0:128], w[lo + 8:lo + 16, 128:256]
            left = [lane(n0, lo + k) for k in range(8)]
            ncols = [lane(n0, lo + 8 + k) for k in range(8)]
        scale = jnp.zeros(wide, F32)
        for k in range(8):
            inv = lax.rsqrt(pivot)
            inv2 = inv * inv
            if k < 7:
                e = line(cols[k + 1], k)
                pivot = line(cols[k + 1], k + 1) - (e * e) * inv2
            elif more:
                e = line(left[7], 0)
                pivot = line(ncols[0], 0) - (e * e) * inv2
            scale = jnp.where(sub == k, inv, scale)
            p0, p1 = line(r0, k), line(r1, k)
            if more:
                m2 = left[k] * inv2
            if k < 7:
                mult = jnp.where(sub > k, cols[k], 0.0) * inv2
                for j in range(k + 1, 8):
                    e = line(cols[j], k)
                    cols[j] = cols[j] - mult * e
                    if more:
                        left[j] = left[j] - m2 * e
                r0 = r0 - mult * p0
                r1 = r1 - mult * p1
            if more:
                for j in range(8):
                    ncols[j] = ncols[j] - m2 * line(left[k], j)
                n0 = n0 - m2 * p0
                n1 = n1 - m2 * p1
        u0, u1 = r0 * scale, r1 * scale
        w[lo:lo + 8, 0:128] = u0
        w[lo:lo + 8, 128:256] = u1
        first = g // 4 * 4
        reach = min(16, first + 6)
        if g + 2 < reach:
            flipped = u0.T
            q0 = [line(u0, k) for k in range(8)]
            q1 = [line(u1, k) for k in range(8)]
            for h in range(8 * g + 16, 8 * reach, 8):
                a0, a1 = w[h:h + 8, 0:128], w[h:h + 8, 128:256]
                for k in range(8):
                    m = jnp.broadcast_to(flipped[h:h + 8, k:k + 1], wide)
                    a0 = a0 - m * q0[k]
                    a1 = a1 - m * q1[k]
                w[h:h + 8, 0:128] = a0
                w[h:h + 8, 128:256] = a1
        if g == first + 3 and reach < 16:
            panel = w[8 * first:8 * first + 32, :]
            change = dot(panel[:, 0:128], panel, 0, 0, HI)
            w[8 * reach:128, :] = w[8 * reach:128, :] - change[8 * reach:128, :]
        if more:
            r0, r1, cols = n0, n1, ncols


def panel_step(colloc, bc, factor, bf, lower, panel, acc, sb, s, t, w, r, bca, bfa, tall, wide, part, theirs,
               dpart, rcore, dacc, ry, s2, rz, lry, ls2, lrz,
               ls, zr, zs, xr, xs, cs, cr, ys, yr, hs, hr, pr, ps, ar, as_, dr, ds, gr, gs, er, es, fs, fr,
               lys, lyr, lhs, lhr):
    g = lax.axis_index("grp")
    d = lax.axis_index("dev")
    y, zh, c = g // 4, (g // 2) % 2, g % 2
    x, zl = d // 8, d % 8
    sent = []

    local = [
        pltpu.make_async_copy(bc, bca.at[d], ls.at[0]),
        pltpu.make_async_copy(bf, bfa.at[d], ls.at[1]),
        pltpu.make_async_copy(colloc, tall, ls.at[2]),
        pltpu.make_async_copy(factor, wide, ls.at[3]),
    ]
    for copy in local:
        copy.start()

    def push(src, dst, ssem, rsem, to, when=None):
        def make():
            return pltpu.make_async_remote_copy(
                src_ref=src(), dst_ref=dst(), send_sem=ssem, recv_sem=rsem, device_id=to(), device_id_type=MESH
            )

        if when is None:
            make().start()
        else:
            pl.when(when)(lambda: make().start())
        sent.append((when, make))

    def arrived(ref, ssem, rsem, when=None):
        def wait():
            pltpu.make_async_remote_copy(
                src_ref=ref, dst_ref=ref, send_sem=ssem, recv_sem=rsem,
                device_id=place(x, y, zl, zh, 1 - c), device_id_type=MESH,
            ).wait_recv()

        if when is None:
            wait()
        else:
            pl.when(when)(wait)

    barrier = pltpu.get_barrier_semaphore()
    ring = [(zl + k % 8) % 8 for k in range(16)]
    half = [(zh + k // 8) % 2 for k in range(16)]
    peers = [place(x, y, zl, zh, 1 - c)]
    peers += [place(x, y, ring[k], half[k], c) for k in range(1, 16)]
    peers += [place((x + k) % 4, y, zl, zh, c) for k in range(1, 4)]
    peers += [place(x, (y + k) % 4, zl, zh, c) for k in range(1, 4)]
    for peer in peers:
        pl.semaphore_signal(barrier, inc=1, device_id=peer, device_id_type=MESH)
    pl.semaphore_wait(barrier, len(peers))

    chunks = [
        (bc, lambda slot: bca.at[slot]),
        (bf.at[0:16], lambda slot: bfa.at[slot, 0:16]),
        (bf.at[16:32], lambda slot: bfa.at[slot, 16:32]),
    ]
    whole = [(bc, lambda slot: bca.at[slot]), (bf, lambda slot: bfa.at[slot])]
    over = [lambda: place((x + 1) % 4, y, zl, zh, c), lambda: place((x + 3) % 4, y, zl, zh, c)]

    def to_x(src, own, when=None):
        for q, (mine, at) in enumerate(whole):
            for way in range(2):
                source = (lambda mine=mine: mine) if own else (lambda at=at: at(x * 8 + src))
                push(source, lambda at=at: at(x * 8 + src), xs.at[way, q, src], xr.at[way, q, src], over[way], when)

    def from_x(src):
        for q, (_, at) in enumerate(whole):
            for way in range(2):
                slot = ((x + 3 + 2 * way) % 4) * 8 + src
                arrived(at(slot), xs.at[way, q, src], xr.at[way, q, src])
                push(lambda at=at, slot=slot: at(slot), lambda at=at, slot=slot: at(slot),
                     xs.at[2, q, src], xr.at[2, q, src], over[way], (src % 2) == way)

    def from_far(src):
        for q, (_, at) in enumerate(whole):
            arrived(at(((x + 2) % 4) * 8 + src), xs.at[2, q, src], xr.at[2, q, src])

    for q, (own, at) in enumerate(chunks):
        for way, step in ((0, 1), (1, -1)):
            ok = (zl < 7) if step == 1 else (zl > 0)
            push(lambda own=own: own, lambda at=at: at(d), zs.at[q, 0, way], zr.at[q, zl],
                 lambda step=step: place(x, y, zl + step, zh, c), ok)
    to_x(zl, True)
    for hop in range(1, 8):
        for q, (own, at) in enumerate(chunks):
            for way, step in ((0, 1), (1, -1)):
                src = zl - step * hop
                inside = (src >= 0) if step == 1 else (src <= 7)
                more = (zl < 7) if step == 1 else (zl > 0)

                @pl.when(inside)
                def _(at=at, src=src, q=q):
                    arrived(at(x * 8 + src), zs.at[q, 0, 0], zr.at[q, src])

                if hop < 7:
                    push(lambda at=at, src=src: at(x * 8 + src), lambda at=at, src=src: at(x * 8 + src),
                         zs.at[q, hop, way], zr.at[q, src],
                         lambda step=step: place(x, y, zl + step, zh, c), jnp.logical_and(inside, more))
        for step in (1, -1):
            src = zl - step * hop
            to_x(src, False, (src >= 0) if step == 1 else (src <= 7))
        if hop == 2:
            from_x(zl)
    mine = pl.ds(x * 8, 8)
    local[0].wait()
    local[1].wait()
    from_far(zl)
    rows = [a * 8 + zl for a in range(4)]
    gram = dot(jnp.concatenate([bca[i] for i in rows], axis=0), bca[mine].reshape(256, 500), 1, 1)
    update = dot(jnp.concatenate([bfa[i] for i in rows], axis=0), bfa[mine].reshape(256, 512), 1, 1, HI)
    for a in range(4):
        for b in range(2):
            for e in range(2):
                lo = a * 32 + b * 16 + e * 8
                dpart[b, a, e, 0] = gram[lo:lo + 8]
                dpart[b, a, e, 1] = update[lo:lo + 8]
    push(lambda: dpart.at[1 - c], lambda: rcore, cs, cr, lambda: place(x, y, zl, zh, 1 - c))
    for k in range(1, 8):
        from_x((zl + k) % 8)
    arrived(rcore, cs, cr)
    dacc[...] = dpart[c] + rcore[...]
    for k in range(1, 4):
        push(lambda k=k: dacc.at[(y + k) % 4], lambda k=k: ry.at[k - 1], ys.at[k - 1], yr.at[k - 1],
             lambda k=k: place(x, (y + k) % 4, zl, zh, c))
    for k in range(1, 4):
        arrived(ry.at[k - 1], ys.at[k - 1], yr.at[k - 1])
    s2[...] = dacc[y] + ry[0] + ry[1] + ry[2]
    push(lambda: s2.at[1 - zh], lambda: rz, hs, hr, lambda: place(x, y, zl, 1 - zh, c))
    for k in range(1, 8):
        from_far((zl + k) % 8)
    local[2].wait()
    local[3].wait()
    for b in range(3):
        gram = dot(tall[:, 128 * b:128 * b + 128], bca[...].reshape(1024, 500), 0, 1)
        for n in range(16):
            lo, hi = max(24 * n, 128 * b), min(24 * n + 24, 128 * b + 128)
            if lo < hi:
                part[n % 2, n // 4, (n // 2) % 2, 0, lo - 24 * n:hi - 24 * n] = gram[lo - 128 * b:hi - 128 * b]

    def products(b):
        update = dot(wide[96 * b:96 * b + 96, :], bfa[...].reshape(1024, 512), 1, 1, HI)
        for h in range(2):
            for k in range(2):
                lo = (h * 2 + k) * 24
                part[k, b, h, 1] = update[lo:lo + 24]

    products(0)
    products(1)
    arrived(rz, hs, hr)
    total = s2[zh] + rz[...]
    row = y * 256 + zl * 32 + c * 16 + zh * 8 + lax.broadcasted_iota(jnp.int32, (8, 256), 0)
    col = x * 256 + lax.broadcasted_iota(jnp.int32, (8, 256), 1)
    sb[x, y, c, zl, zh] = total[0] * total[0] + jnp.where(row == col, F32(DAMPING), F32(0.0)) - total[1]
    for k in range(1, 16):
        push(lambda: sb.at[x, y, c, zl, zh], lambda: sb.at[x, y, c, zl, zh], ps.at[k - 1], pr.at[k - 1],
             lambda k=k: place(x, y, ring[k], half[k], c), x >= y)
    products(2)
    products(3)
    push(lambda: part.at[1 - c], lambda: theirs, fs, fr, lambda: place(x, y, zl, zh, 1 - c))
    for k in range(1, 16):
        back_l, back_h = (zl + 8 - k % 8) % 8, (zh + k // 8) % 2
        arrived(sb.at[x, y, c, back_l, back_h], ps.at[k - 1], pr.at[k - 1], x >= y)
    first = lambda k: ((x + (1 - c) * k) % 4, (y + c * k) % 4)
    second = lambda k: ((x + c * k) % 4, (y + (1 - c) * k) % 4)

    def core_copy(n, bx, by):
        push(lambda: sb.at[bx, by, c], lambda: sb.at[bx, by, c], es.at[n], er.at[n],
             lambda: place(x, y, zl, zh, 1 - c), bx >= by)

    for k in range(1, 4):
        push(lambda: sb.at[x, y, c], lambda: sb.at[x, y, c], as_.at[k - 1], ar.at[k - 1],
             lambda k=k: place(*first(k), zl, zh, c), x >= y)
    order = []
    beside = [lambda: place(*second(1), zl, zh, c), lambda: place(*second(3), zl, zh, c)]
    for m in range(4):
        bx, by = first(4 - m) if m else (x, y)
        if m:
            arrived(sb.at[bx, by, c], as_.at[m - 1], ar.at[m - 1], bx >= by)
        for way in range(2):
            push(lambda bx=bx, by=by: sb.at[bx, by, c], lambda bx=bx, by=by: sb.at[bx, by, c],
                 ds.at[m, way], dr.at[m, way], beside[way], bx >= by)
        core_copy(m, bx, by)
        order.append((bx, by))
    shifted = lambda m, k: ((order[m][0] + c * k) % 4, (order[m][1] + (1 - c) * k) % 4)
    for m in range(4):
        for way in range(2):
            bx, by = shifted(m, 3 - 2 * way)
            arrived(sb.at[bx, by, c], ds.at[m, way], dr.at[m, way], bx >= by)
            part_of = lambda bx=bx, by=by, way=way: sb.at[bx, by, c, way * 4:way * 4 + 4]
            push(part_of, part_of, gs.at[m, way], gr.at[m, way], beside[way], bx >= by)
            core_copy(4 + (8 * way) + m, bx, by)
    arrived(theirs, fs, fr)
    for b in range(4):
        acc[b] = part[c, b] + theirs[b]
    for m in range(4):
        bx, by = shifted(m, 2)
        for way in range(2):
            arrived(sb.at[bx, by, c, way * 4:way * 4 + 4], gs.at[m, way], gr.at[m, way], bx >= by)
        core_copy(8 + m, bx, by)
    def half_copy():
        return pltpu.make_async_remote_copy(
            src_ref=ls2.at[1 - zh], dst_ref=lrz, send_sem=lhs, recv_sem=lhr,
            device_id=place(x, y, zl, 1 - zh, c), device_id_type=MESH,
        )


    def across_cores(row_block):
        for n in range(16):
            m, k = n % 4, n // 4
            bx = (x + 8 - (c * m + (1 - c) * k)) % 4
            by = (y + 8 - ((1 - c) * m + c * k)) % 4
            arrived(sb.at[bx, by, 1 - c], es.at[n], er.at[n], jnp.logical_and(by == row_block, bx >= by))

    for k in range(1, 4):
        push(lambda k=k: acc.at[(y + k) % 4], lambda k=k: lry.at[k - 1], lys.at[k - 1], lyr.at[k - 1],
             lambda k=k: place(x, (y + k) % 4, zl, zh, c))
    s[256:, :] = jnp.zeros((768, 1024), F32)

    def load(b):
        across_cores(b)

        def some(i, _):
            for k in range(2):
                for h in range(2):
                    at = pl.ds(pl.multiple_of(b * 256 + i * 32 + k * 16 + h * 8, 8), 8)
                    for a in range(b, 4):
                        span = slice(a * 256, a * 256 + 256)
                        if b == 0:
                            s[at, span] = sb[a, b, k, i, h]
                        else:
                            s[at, span] = s[at, span] + sb[a, b, k, i, h]
            return 0

        lax.fori_loop(0, 8, some, 0)

    load(0)
    row = lax.broadcasted_iota(jnp.int32, (128, 128), 0)
    col = lax.broadcasted_iota(jnp.int32, (128, 128), 1)
    eye = jnp.where(row == col, F32(1.0), F32(0.0))

    def block(j, _):
        for b in range(1, 4):
            pl.when(j == 2 * b)(functools.partial(load, b))

        dj = pl.ds(pl.multiple_of(j * 128, 128), 128)
        w[:, 0:128] = s[dj, dj]
        w[:, 128:256] = eye
        diagonal(w)
        t[dj, :] = w[:, 128:256]

        def across(k, _):
            dk = pl.ds(pl.multiple_of(k * 256, 256), 256)
            s[dj, dk] = dot(t[dj, :], s[dj, dk], 1, 0, HI)
            return 0

        lax.fori_loop((j + 1) // 2, 4, across, 0)
        s[dj, dj] = jnp.where(col >= row, w[:, 0:128], 0.0)

        def update(rows, start):
            left = s[dj, rows]

            def tile(k, _):
                dk = pl.ds(pl.multiple_of(k * 256, 256), 256)
                s[rows, dk] = s[rows, dk] - dot(left, s[dj, dk], 0, 0, HI)
                return 0

            lax.fori_loop(start, 4, tile, 0)

        @pl.when(j % 2 == 0)
        def _():
            update(pl.ds(pl.multiple_of(jnp.minimum(j + 1, 7) * 128, 128), 128), j // 2)

        def trailing(i, _):
            update(pl.ds(pl.multiple_of(i * 256, 256), 256), i)
            return 0

        lax.fori_loop(j // 2 + 1, 4, trailing, 0)

        @pl.when(j == 2)
        def _():
            for k in range(1, 4):
                arrived(lry.at[k - 1], lys.at[k - 1], lyr.at[k - 1])
            ls2[...] = acc[y] + lry[0] + lry[1] + lry[2]
            half_copy().start()

        return 0

    lax.fori_loop(0, 8, block, 0)
    half_copy().wait()
    gram = ls2[zh, 0] + lrz[0]
    r[...] = gram * gram - (ls2[zh, 1] + lrz[1])
    for j in range(8):
        a, b = j * 128, j * 128 + 128
        xj = dot(r[:, a:b], t[a:b, :], 1, 1, HI)
        panel[0, :, a:b] = xj
        if j < 7:
            r[:, b:] = r[:, b:] - dot(xj, s[a:b, b:], 1, 0, HI)
    tile = pl.ds(pl.multiple_of((d // 4) * 128, 128), 128)
    for j in range(8):
        flipped = s[j * 128:j * 128 + 128, tile].T
        for q in range(4):
            @pl.when(d % 4 == q)
            def _(q=q):
                lower[:, j * 128:j * 128 + 128] = jnp.where(d // 4 >= j, flipped[q * 32:q * 32 + 32, :], 0.0)
    for when, make in sent:
        if when is None:
            make().wait_send()
        else:
            pl.when(when)(lambda make=make: make().wait_send())


def whole_step(colloc, bc, factor, bf):
    D = pltpu.SemaphoreType.DMA
    whole = pl.BlockSpec(memory_space=pltpu.MemorySpace.HBM)
    return pl.pallas_call(
        panel_step,
        out_shape=[
            jax.ShapeDtypeStruct((32, 1024), F32),
            jax.ShapeDtypeStruct((1, 24, 1024), F32),
        ],
        in_specs=[whole] * 4,
        out_specs=[VMEM] * 2,
        scratch_shapes=[
            pltpu.VMEM((4, 2, 2, 24, 1024), F32),
            pltpu.VMEM((4, 4, 2, 8, 2, 8, 256), F32),
            pltpu.VMEM((1024, 1024), F32),
            pltpu.VMEM((1024, 128), F32),
            pltpu.VMEM((128, 256), F32),
            pltpu.VMEM((24, 1024), F32),
            pltpu.VMEM((32, 32, 500), jnp.bfloat16),
            pltpu.VMEM((32, 32, 512), F32),
            pltpu.VMEM((500, 384), jnp.bfloat16),
            pltpu.VMEM((384, 512), F32),
            pltpu.VMEM((2, 4, 2, 2, 24, 1024), F32),
            pltpu.VMEM((4, 2, 2, 24, 1024), F32),
            pltpu.VMEM((2, 4, 2, 2, 8, 256), F32),
            pltpu.VMEM((4, 2, 2, 8, 256), F32),
            pltpu.VMEM((4, 2, 2, 8, 256), F32),
            pltpu.VMEM((3, 2, 2, 8, 256), F32),
            pltpu.VMEM((2, 2, 8, 256), F32),
            pltpu.VMEM((2, 8, 256), F32),
            pltpu.VMEM((3, 2, 2, 24, 1024), F32),
            pltpu.VMEM((2, 2, 24, 1024), F32),
            pltpu.VMEM((2, 24, 1024), F32),
            D((4,)), D((3, 8)), D((3, 7, 2)), D((3, 2, 8)), D((3, 2, 8)),
            D, D, D((3,)), D((3,)), D, D, D((15,)), D((15,)), D((3,)), D((3,)),
            D((4, 2)), D((4, 2)), D((4, 2)), D((4, 2)), D((16,)), D((16,)), D, D,
            D((3,)), D((3,)), D, D,
        ],
        compiler_params=pltpu.CompilerParams(collective_id=0, has_side_effects=True, vmem_limit_bytes=60 * 2**20),
        name="panel_step",
    )(colloc, bc, factor, bf)


def on_device(colloc, block_colloc, factor, block_factor):
    return tuple(whole_step(colloc.T, block_colloc, factor, block_factor))


def solution(mesh):
    placed = (P("dev", "grp"), P("dev", "grp"), P("dev", "grp"), P("dev", "grp"))
    return jax.shard_map(
        on_device,
        mesh=mesh,
        in_specs=placed,
        out_specs=(P("dev", None), P("dev", "grp", None)),
        check_vma=False,
    )
```

time: 152 us -> 147 us (0.967)
  the two profiles are of different devices: /device:TPU:25 before, /device:TPU:28 now
where the time goes in v5:
time: 147 us
  Pallas kernels  144 us (98%)
  local copies, waits for them, and re-layouts  2.25 us (2%)
    pallas_call x1, Pallas kernels, whole_step(): pl.pallas_call(panel_step, out_shape=[jax.ShapeDtypeStruct((32, 1024), F3...  144 us

profile of v5, /device:TPU:28, one launch (start us, length us, event | category | flops | bytes accessed | tf_op | source)
XLA Modules:
  0.0 147.3 jit_solution(6420923312736212530)
XLA Ops:
  0.6 144.4 %panel_step.1 = (f32[32,1024]{1,0:T(8,128)}, f32[1,24,1024]{2,1,0:T(8,128)}) custom-call(bf16[500,384]{1,0:T(8,128)(2,1)} %bitcast.1, bf16[32,500]{1,0:T(8,128)(2,1)} %bc.1, f32[384,512]{1,0:T(8,128)} %factor.1, f32[32,512]{1,0:T(8,128)} %bf.1), custom_call_target="tpu_custom_call" | custom-call | tf_op jit(solution)/shard_map/panel_step/pallas_call | solution.py:410
  145.0 0.0 copy-start
  145.0 1.6 %copy.8 = f32[32,1024]{1,0:T(8,128)} copy(f32[32,1024]{1,0:T(8,128)} %get-tuple-element.4) | data formatting | bytes 262144
  146.6 0.0 copy-done
  146.6 0.6 copy.9
Async XLA Ops:
  145.0 1.6 %copy-start = (f32[1,24,1024]{2,1,0:T(8,128)S(1)}, f32[1,24,1024]{2,1,0:T(8,128)}, u32[]{:S(2)}) copy-start(f32[1,24,1024]{2,1,0:T(8,128)} %get-tuple-element.5) | copy-start | bytes 294916

commit v6 on v5

--- a/solution.py
+++ b/solution.py
@@ -91,7 +91,7 @@
 
 
 def panel_step(colloc, bc, factor, bf, lower, panel, acc, sb, s, t, w, r, bca, bfa, tall, wide, part, theirs,
-               dpart, rcore, dacc, ry, s2, rz, lry, ls2, lrz,
+               dpart, rcore, dacc, ry, s2, rz, lone, lfwd, ltwo, ls2, lrz,
                ls, zr, zs, xr, xs, cs, cr, ys, yr, hs, hr, pr, ps, ar, as_, dr, ds, gr, gs, er, es, fs, fr,
                lys, lyr, lhs, lhr):
     g = lax.axis_index("grp")
@@ -306,9 +306,23 @@
             by = (y + 8 - ((1 - c) * m + c * k)) % 4
             arrived(sb.at[bx, by, 1 - c], es.at[n], er.at[n], jnp.logical_and(by == row_block, bx >= by))
 
-    for k in range(1, 4):
-        push(lambda k=k: acc.at[(y + k) % 4], lambda k=k: lry.at[k - 1], lys.at[k - 1], lyr.at[k - 1],
-             lambda k=k: place(x, (y + k) % 4, zl, zh, c))
+    pair, mirror = y + 1 - 2 * (y % 2), 3 - y
+    meet = [(pair, mirror), (mirror, pair)]
+
+    def y_copy(src, dst, n, to):
+        return pltpu.make_async_remote_copy(
+            src_ref=src, dst_ref=dst, send_sem=lys.at[n], recv_sem=lyr.at[n],
+            device_id=place(x, to, zl, zh, c), device_id_type=MESH,
+        )
+
+    def one(i, k):
+        near, far = meet[i]
+        beyond = 3 - near if i == 0 else near + 1 - 2 * (near % 2)
+        return y_copy(acc.at[near if k == 0 else beyond, i], lone.at[i, k], 2 * i + k, near)
+
+    def two(i):
+        return y_copy(lfwd.at[i], ltwo.at[i], 4 + i, meet[i][1])
+
     s[256:, :] = jnp.zeros((768, 1024), F32)
 
     def load(b):
@@ -371,11 +385,25 @@
 
         lax.fori_loop(j // 2 + 1, 4, trailing, 0)
 
-        @pl.when(j == 2)
+        @pl.when(j == 1)
         def _():
-            for k in range(1, 4):
-                arrived(lry.at[k - 1], lys.at[k - 1], lyr.at[k - 1])
-            ls2[...] = acc[y] + lry[0] + lry[1] + lry[2]
+            for i in range(2):
+                for k in range(2):
+                    one(i, k).start()
+
+        @pl.when(j == 3)
+        def _():
+            for i in range(2):
+                for k in range(2):
+                    one(i, k).wait()
+                lfwd[i] = acc[meet[i][1], i] + lone[i, 1]
+                two(i).start()
+
+        @pl.when(j == 4)
+        def _():
+            for i in range(2):
+                two(i).wait()
+                ls2[i] = acc[y, i] + lone[i, 0] + ltwo[i]
             half_copy().start()
 
         return 0
@@ -434,13 +462,15 @@
             pltpu.VMEM((3, 2, 2, 8, 256), F32),
             pltpu.VMEM((2, 2, 8, 256), F32),
             pltpu.VMEM((2, 8, 256), F32),
-            pltpu.VMEM((3, 2, 2, 24, 1024), F32),
+            pltpu.VMEM((2, 2, 2, 24, 1024), F32),
+            pltpu.VMEM((2, 2, 24, 1024), F32),
+            pltpu.VMEM((2, 2, 24, 1024), F32),
             pltpu.VMEM((2, 2, 24, 1024), F32),
             pltpu.VMEM((2, 24, 1024), F32),
             D((4,)), D((3, 8)), D((3, 7, 2)), D((3, 2, 8)), D((3, 2, 8)),
             D, D, D((3,)), D((3,)), D, D, D((15,)), D((15,)), D((3,)), D((3,)),
             D((4, 2)), D((4, 2)), D((4, 2)), D((4, 2)), D((16,)), D((16,)), D, D,
-            D((3,)), D((3,)), D, D,
+            D((6,)), D((6,)), D, D,
         ],
         compiler_params=pltpu.CompilerParams(collective_id=0, has_side_effects=True, vmem_limit_bytes=60 * 2**20),
         name="panel_step",

time: 147 us -> 150 us (1.020)
  the two profiles are of different devices: /device:TPU:28 before, /device:TPU:25 now
where the time goes in v6:
time: 150 us; the launch traced here: 149 us
  Pallas kernels  146 us (97%)
  local copies, waits for them, and re-layouts  2.25 us (2%)
    pallas_call x1, Pallas kernels, whole_step(): pl.pallas_call(panel_step, out_shape=[jax.ShapeDtypeStruct((32, 1024), F3...  146 us

profile of v6, /device:TPU:25, one launch (start us, length us, event | category | flops | bytes accessed | tf_op | source)
XLA Modules:
  0.0 148.8 jit_solution(8015081847560480060)
XLA Ops:
  0.6 146.0 %panel_step.1 = (f32[32,1024]{1,0:T(8,128)}, f32[1,24,1024]{2,1,0:T(8,128)}) custom-call(bf16[500,384]{1,0:T(8,128)(2,1)} %bitcast.1, bf16[32,500]{1,0:T(8,128)(2,1)} %bc.1, f32[384,512]{1,0:T(8,128)} %factor.1, f32[32,512]{1,0:T(8,128)} %bf.1), custom_call_target="tpu_custom_call" | custom-call | tf_op jit(solution)/shard_map/panel_step/pallas_call | solution.py:438
  146.6 0.0 copy-start
  146.6 1.6 %copy.8 = f32[32,1024]{1,0:T(8,128)} copy(f32[32,1024]{1,0:T(8,128)} %get-tuple-element.4) | data formatting | bytes 262144
  148.2 0.0 copy-done
  148.2 0.6 copy.9
Async XLA Ops:
  146.6 1.6 %copy-start = (f32[1,24,1024]{2,1,0:T(8,128)S(1)}, f32[1,24,1024]{2,1,0:T(8,128)}, u32[]{:S(2)}) copy-start(f32[1,24,1024]{2,1,0:T(8,128)} %get-tuple-element.5) | copy-start | bytes 294916
